TPU v7x, 32 devices: a whole 2x2x4 slice. The times are simulated.
32 devices in a mesh: dp: 8 (over y, x, core), fsdp: 4 (over z).
Axes of the slice: x: 2, y: 2, z: 4, core: 2. Of those that a mesh axis runs over, the one named last changes fastest.
Arguments:
- inputs: bfloat16 [32768, 960], P(('dp', 'fsdp')), may hold values from -6 to 6
- w_query: bfloat16 [960, 960], P('fsdp'), may hold values from -0.1875 to 0.1875
- w_key: bfloat16 [960, 320], P('fsdp'), may hold values from -0.1875 to 0.1875
- w_value: bfloat16 [960, 320], P('fsdp'), may hold values from -0.1875 to 0.1875
- w_out: bfloat16 [960, 960], P('fsdp'), may hold values from -1 to 1
- w_gate: bfloat16 [960, 2560], P('fsdp'), may hold values from -0.1875 to 0.1875
- w_up: bfloat16 [960, 2560], P('fsdp'), may hold values from -0.1875 to 0.1875
- w_down: bfloat16 [2560, 960], P('fsdp'), may hold values from -0.125 to 0.125
- gain_attn: bfloat16 [960], P('fsdp'), may hold values from 0.5 to 1.5
- gain_ffn: bfloat16 [960], P('fsdp'), may hold values from 0.5 to 1.5
- w_router: bfloat16 [960, 3], P('fsdp'), may hold values from -0.125 to 0.125
- seq_start: int32 [32768], P(('dp', 'fsdp')), may hold values from 0 to 768, as said below
- pick_first: int32 [24576], P(('dp', 'fsdp')), may hold values from 0 to 1023, as said below
- pick_second: int32 [16384], P(('dp', 'fsdp')), may hold values from 0 to 1023, as said below
- pick_third: int32 [8192], P(('dp', 'fsdp')), may hold values from 0 to 1023, as said below
- out_grad: bfloat16 [32768, 960], P(('dp', 'fsdp')), may hold values from -6 to 6
Outputs:
- hidden_out: bfloat16 [32768, 960], P(('dp', 'fsdp'))
- grad_inputs: bfloat16 [32768, 960], P(('dp', 'fsdp'))
- grad_query: float32 [960, 960], P('fsdp')
- grad_key: float32 [960, 320], P('fsdp')
- grad_value: float32 [960, 320], P('fsdp')
- grad_out: float32 [960, 960], P('fsdp')
- grad_gate: float32 [960, 2560], P('fsdp')
- grad_up: float32 [960, 2560], P('fsdp')
- grad_down: float32 [2560, 960], P('fsdp')
- grad_gain_attn: float32 [960], P('fsdp')
- grad_gain_ffn: float32 [960], P('fsdp')
- grad_router: float32 [960, 3], P('fsdp')
Inputs may be any that keep to these rules, and one draw needn't show every extreme that they name: Within each group of 1024 tokens either all tokens form one sequence (seq_start 0) or four sequences of 256 tokens; a third of the groups, rounded down, hold one sequence. `pick_first`: per group, 768 distinct ascending indices below 1024. `pick_second`: per group, 512 distinct ascending indices, all among the group's pick_first. `pick_third`: per group, 256 distinct ascending indices, all among the group's pick_second.
All inputs are finite; a program needn't handle non-finite values.
Results may differ from a plain program's by a relative error of at most 0.025.
Values may be sent and summed in bfloat16 or wider, within the bound.
A program may use at most 256 MiB of HBM per device.

v0:
```python
import math

import jax
import jax.numpy as jnp
from jax import lax
from jax.sharding import PartitionSpec as P

HEADS = 15
KV_HEADS = 5
HEAD_DIM = 64
NREC = 3


norm_eps = 1e-05
masked_score = -1e30
highest = lax.Precision.HIGHEST


def low_dot(spec, left, right):
    return jnp.einsum(spec, left, right, preferred_element_type=jnp.float32)


def rms_norm(values, gain):
    return values * lax.rsqrt(jnp.mean(values * values, axis=-1, keepdims=True) + norm_eps) * gain


def rms_back(values, gain, grad):
    _, pullback = jax.vjp(rms_norm, values, gain)
    return pullback(grad)


def rotary(values, positions, head_count):
    half_dim = HEAD_DIM // 2
    frequency = jnp.exp(
        jnp.arange(half_dim, dtype=jnp.float32) * (-2.0 * math.log(10000.0) / HEAD_DIM)
    )
    angles = positions.astype(jnp.float32)[:, None] * frequency[None, :]
    cosine_table = jnp.cos(angles)[:, None, :]
    sine_table = jnp.sin(angles)[:, None, :]
    shaped = values.reshape(values.shape[0], head_count, HEAD_DIM)
    first_half = shaped[..., :half_dim]
    second_half = shaped[..., half_dim:]
    turned = jnp.concatenate(
        [
            first_half * cosine_table - second_half * sine_table,
            second_half * cosine_table + first_half * sine_table,
        ],
        axis=-1,
    )
    return turned.reshape(values.shape[0], head_count * HEAD_DIM)


def rotary_back(grad, positions, head_count):
    _, pullback = jax.vjp(lambda values: rotary(values, positions, head_count), grad)
    return pullback(grad)[0]


def split_groups(queries, keys_turned, values):
    row_count = queries.shape[0]
    group_size = HEADS // KV_HEADS
    return (
        queries.reshape(row_count, KV_HEADS, group_size, HEAD_DIM).transpose(1, 2, 0, 3),
        keys_turned.reshape(row_count, KV_HEADS, HEAD_DIM).transpose(1, 0, 2),
        values.reshape(row_count, KV_HEADS, HEAD_DIM).transpose(1, 0, 2),
    )


def group_scores(query_head, key_head, allowed):
    raw_scores = low_dot("gqd,kd->gqk", query_head, key_head)
    return jnp.where(allowed[None], raw_scores * (1.0 / math.sqrt(HEAD_DIM)), masked_score)


def attend_forward(queries, keys_turned, values, allowed):
    query_groups, key_groups, value_groups = split_groups(queries, keys_turned, values)

    def one_group(operands):
        query_head, key_head, value_head = operands
        scores = group_scores(query_head, key_head, allowed)
        top_score = jnp.max(scores, axis=-1, keepdims=True)
        weights = jnp.exp(scores - top_score)
        totals = jnp.sum(weights, axis=-1, keepdims=True)
        probabilities = (weights / totals).astype(jnp.bfloat16)
        return (low_dot("gqk,kd->gqd", probabilities, value_head), top_score, totals)

    mixed, top_score, totals = lax.map(one_group, (query_groups, key_groups, value_groups))
    row_count = queries.shape[0]
    return (mixed.transpose(2, 0, 1, 3).reshape(row_count, HEADS * HEAD_DIM), top_score, totals)


def attend_backward(queries, keys_turned, values, allowed, top_score, totals, grad_mixed):
    query_groups, key_groups, value_groups = split_groups(queries, keys_turned, values)
    row_count = queries.shape[0]
    group_size = HEADS // KV_HEADS
    grad_groups = grad_mixed.reshape(row_count, KV_HEADS, group_size, HEAD_DIM).transpose(
        1, 2, 0, 3
    )
    score_scale = 1.0 / math.sqrt(HEAD_DIM)

    def one_group(operands):
        query_head, key_head, value_head, top_head, total_head, grad_head = operands
        scores = group_scores(query_head, key_head, allowed)
        probabilities = jnp.exp(scores - top_head) / total_head
        grad_probs = low_dot("gqd,kd->gqk", grad_head, value_head)
        grad_value = low_dot("gqk,gqd->kd", probabilities.astype(jnp.bfloat16), grad_head)
        inner_sum = jnp.sum(probabilities * grad_probs, axis=-1, keepdims=True)
        grad_scores = (probabilities * (grad_probs - inner_sum)).astype(jnp.bfloat16)
        grad_query = low_dot("gqk,kd->gqd", grad_scores, key_head) * score_scale
        grad_key = low_dot("gqk,gqd->kd", grad_scores, query_head) * score_scale
        return (grad_query, grad_key, grad_value)

    query_part, key_part, value_part = lax.map(
        one_group, (query_groups, key_groups, value_groups, top_score, totals, grad_groups)
    )
    return (
        query_part.transpose(2, 0, 1, 3).reshape(row_count, HEADS * HEAD_DIM),
        key_part.transpose(1, 0, 2).reshape(row_count, KV_HEADS * HEAD_DIM),
        value_part.transpose(1, 0, 2).reshape(row_count, KV_HEADS * HEAD_DIM),
    )


def forward_step(hidden, seq_start, token_index, gathered, section):
    w_query, w_key, w_value, w_out, w_gate, w_up, w_down, gain_attn, gain_ffn, w_router = gathered
    token_rows = jnp.take(hidden, token_index, axis=0)
    begins = jnp.take(seq_start, token_index)
    positions = token_index - begins
    allowed = (token_index[None, :] <= token_index[:, None]) & (
        begins[:, None] <= token_index[None, :]
    )
    normed = rms_norm(token_rows, gain_attn.astype(jnp.float32)).astype(jnp.bfloat16)
    queries = rotary(low_dot("kd,de->ke", normed, w_query), positions, HEADS).astype(jnp.bfloat16)
    keys_turned = rotary(low_dot("kd,de->ke", normed, w_key), positions, KV_HEADS).astype(
        jnp.bfloat16
    )
    values = low_dot("kd,de->ke", normed, w_value).astype(jnp.bfloat16)
    mixed, top_score, totals = attend_forward(queries, keys_turned, values, allowed)
    mixed_low = mixed.astype(jnp.bfloat16)
    attn_branch = low_dot("ke,ed->kd", mixed_low, w_out)
    middle = token_rows + attn_branch
    inner = rms_norm(middle, gain_ffn.astype(jnp.float32)).astype(jnp.bfloat16)
    gate_pre = low_dot("kd,df->kf", inner, w_gate)
    up_pre = low_dot("kd,df->kf", inner, w_up)
    activated = (gate_pre * jax.nn.sigmoid(gate_pre) * up_pre).astype(jnp.bfloat16)
    ffn_branch = low_dot("kf,fd->kd", activated, w_down)
    router_gate = jax.nn.sigmoid(
        jnp.dot(token_rows, w_router[:, section].astype(jnp.float32), precision=highest)
    )
    branches = attn_branch + ffn_branch
    hidden = hidden.at[token_index].set(token_rows + router_gate[:, None] * branches)
    kept_state = (
        token_index,
        positions,
        allowed,
        token_rows,
        normed,
        queries,
        keys_turned,
        values,
        top_score,
        totals,
        mixed_low,
        middle,
        inner,
        gate_pre,
        up_pre,
        activated,
        router_gate,
        branches,
    )
    return (hidden, kept_state)


def backward_step(grad_hidden, kept_state, gathered, section):
    w_query, w_key, w_value, w_out, w_gate, w_up, w_down, gain_attn, gain_ffn, w_router = gathered
    (
        token_index,
        positions,
        allowed,
        token_rows,
        normed,
        queries,
        keys_turned,
        values,
        top_score,
        totals,
        mixed_low,
        middle,
        inner,
        gate_pre,
        up_pre,
        activated,
        router_gate,
        branches,
    ) = kept_state
    router_column = w_router[:, section].astype(jnp.float32)
    grad_new = jnp.take(grad_hidden, token_index, axis=0)
    grad_logit = jnp.sum(grad_new * branches, axis=1) * router_gate * (1.0 - router_gate)
    router_col_grad = jnp.dot(grad_logit, token_rows, precision=highest)
    grad_rows = grad_new + grad_logit[:, None] * router_column[None, :]
    grad_branch = router_gate[:, None] * grad_new
    grad_ffn = grad_branch.astype(jnp.bfloat16)
    grad_down_w = low_dot("kf,kd->fd", activated, grad_ffn)
    grad_act = low_dot("kd,fd->kf", grad_ffn, w_down)
    sigmoid_gate = jax.nn.sigmoid(gate_pre)
    grad_gate_pre = (
        grad_act * up_pre * (sigmoid_gate + gate_pre * sigmoid_gate * (1.0 - sigmoid_gate))
    ).astype(jnp.bfloat16)
    grad_up_pre = (grad_act * (gate_pre * sigmoid_gate)).astype(jnp.bfloat16)
    grad_gate_w = low_dot("kd,kf->df", inner, grad_gate_pre)
    grad_up_w = low_dot("kd,kf->df", inner, grad_up_pre)
    grad_inner = low_dot("kf,df->kd", grad_gate_pre, w_gate) + low_dot(
        "kf,df->kd", grad_up_pre, w_up
    )
    grad_middle, grad_gain_ffn = rms_back(middle, gain_ffn.astype(jnp.float32), grad_inner)
    grad_attn = (grad_branch + grad_middle).astype(jnp.bfloat16)
    grad_rows = grad_rows + grad_middle
    grad_out_w = low_dot("ke,kd->ed", mixed_low, grad_attn)
    grad_mixed = low_dot("kd,ed->ke", grad_attn, w_out).astype(jnp.bfloat16)
    grad_queries, grad_keys, grad_values = attend_backward(
        queries, keys_turned, values, allowed, top_score, totals, grad_mixed
    )
    grad_query_pre = rotary_back(grad_queries, positions, HEADS).astype(jnp.bfloat16)
    grad_key_pre = rotary_back(grad_keys, positions, KV_HEADS).astype(jnp.bfloat16)
    grad_value_pre = grad_values.astype(jnp.bfloat16)
    grad_query_w = low_dot("kd,ke->de", normed, grad_query_pre)
    grad_key_w = low_dot("kd,ke->de", normed, grad_key_pre)
    grad_value_w = low_dot("kd,ke->de", normed, grad_value_pre)
    grad_normed = (
        low_dot("ke,de->kd", grad_query_pre, w_query)
        + low_dot("ke,de->kd", grad_key_pre, w_key)
        + low_dot("ke,de->kd", grad_value_pre, w_value)
    )
    grad_norm_rows, grad_gain_attn = rms_back(
        token_rows, gain_attn.astype(jnp.float32), grad_normed
    )
    grad_rows = grad_rows + grad_norm_rows
    grad_hidden = grad_hidden.at[token_index].set(grad_rows)
    router_grad = (
        jnp.zeros((token_rows.shape[1], NREC), jnp.float32).at[:, section].set(router_col_grad)
    )
    return (
        grad_hidden,
        (
            grad_query_w,
            grad_key_w,
            grad_value_w,
            grad_out_w,
            grad_gate_w,
            grad_up_w,
            grad_down_w,
            grad_gain_attn,
            grad_gain_ffn,
            router_grad,
        ),
    )


def gather_forward(shards):
    return (
        lax.all_gather(shards[0], "fsdp", axis=0, tiled=True),
        lax.all_gather(shards[1], "fsdp", axis=0, tiled=True),
        lax.all_gather(shards[2], "fsdp", axis=0, tiled=True),
        lax.all_gather(shards[3], "fsdp", axis=0, tiled=True),
        lax.all_gather(shards[4], "fsdp", axis=0, tiled=True),
        lax.all_gather(shards[5], "fsdp", axis=0, tiled=True),
        lax.all_gather(shards[6], "fsdp", axis=0, tiled=True),
        lax.all_gather(shards[7], "fsdp", axis=0, tiled=True),
        lax.all_gather(shards[8], "fsdp", axis=0, tiled=True),
        lax.all_gather(shards[9], "fsdp", axis=0, tiled=True),
    )


def gather_backward(shards):
    return (
        lax.all_gather(shards[0], "fsdp", axis=0, tiled=True),
        lax.all_gather(shards[1], "fsdp", axis=0, tiled=True),
        lax.all_gather(shards[2], "fsdp", axis=0, tiled=True),
        lax.all_gather(shards[3], "fsdp", axis=0, tiled=True),
        lax.all_gather(shards[4], "fsdp", axis=0, tiled=True),
        lax.all_gather(shards[5], "fsdp", axis=0, tiled=True),
        lax.all_gather(shards[6], "fsdp", axis=0, tiled=True),
        lax.all_gather(shards[7], "fsdp", axis=0, tiled=True),
        lax.all_gather(shards[8], "fsdp", axis=0, tiled=True),
        lax.all_gather(shards[9], "fsdp", axis=0, tiled=True),
    )


def reduce_end(summed):
    return (
        lax.psum_scatter(
            summed[0].astype(jnp.bfloat16), "fsdp", scatter_dimension=0, tiled=True
        ).astype(jnp.float32),
        lax.psum_scatter(
            summed[1].astype(jnp.bfloat16), "fsdp", scatter_dimension=0, tiled=True
        ).astype(jnp.float32),
        lax.psum_scatter(
            summed[2].astype(jnp.bfloat16), "fsdp", scatter_dimension=0, tiled=True
        ).astype(jnp.float32),
        lax.psum_scatter(
            summed[3].astype(jnp.bfloat16), "fsdp", scatter_dimension=0, tiled=True
        ).astype(jnp.float32),
        lax.psum_scatter(
            summed[4].astype(jnp.bfloat16), "fsdp", scatter_dimension=0, tiled=True
        ).astype(jnp.float32),
        lax.psum_scatter(
            summed[5].astype(jnp.bfloat16), "fsdp", scatter_dimension=0, tiled=True
        ).astype(jnp.float32),
        lax.psum_scatter(
            summed[6].astype(jnp.bfloat16), "fsdp", scatter_dimension=0, tiled=True
        ).astype(jnp.float32),
        lax.psum_scatter(
            summed[7].astype(jnp.bfloat16), "fsdp", scatter_dimension=0, tiled=True
        ).astype(jnp.float32),
        lax.psum_scatter(
            summed[8].astype(jnp.bfloat16), "fsdp", scatter_dimension=0, tiled=True
        ).astype(jnp.float32),
        lax.psum_scatter(
            summed[9].astype(jnp.bfloat16), "fsdp", scatter_dimension=0, tiled=True
        ).astype(jnp.float32),
    )


def body(
    inputs,
    w_query,
    w_key,
    w_value,
    w_out,
    w_gate,
    w_up,
    w_down,
    gain_attn,
    gain_ffn,
    w_router,
    seq_start,
    pick_first,
    pick_second,
    pick_third,
    out_grad,
):
    shards = (w_query, w_key, w_value, w_out, w_gate, w_up, w_down, gain_attn, gain_ffn, w_router)
    pick_lists = (pick_first, pick_second, pick_third)
    hidden = inputs.astype(jnp.float32)
    gathered = None
    saved_steps = []
    for section in range(NREC):
        gathered = gather_forward(shards)
        hidden, kept_state = forward_step(hidden, seq_start, pick_lists[section], gathered, section)
        saved_steps.append(kept_state)
    result = hidden.astype(jnp.bfloat16)
    grad_hidden = out_grad.astype(jnp.float32)
    summed = None
    shares = None
    for section in reversed(range(NREC)):
        gathered = gather_backward(shards)
        grad_hidden, step_grads = backward_step(
            grad_hidden, saved_steps[section], gathered, section
        )
        summed = step_grads if summed is None else jax.tree.map(jnp.add, summed, step_grads)
    shares = reduce_end(summed)
    totals = (
        lax.psum(shares[0].astype(jnp.bfloat16), "dp").astype(jnp.float32),
        lax.psum(shares[1].astype(jnp.bfloat16), "dp").astype(jnp.float32),
        lax.psum(shares[2].astype(jnp.bfloat16), "dp").astype(jnp.float32),
        lax.psum(shares[3].astype(jnp.bfloat16), "dp").astype(jnp.float32),
        lax.psum(shares[4].astype(jnp.bfloat16), "dp").astype(jnp.float32),
        lax.psum(shares[5].astype(jnp.bfloat16), "dp").astype(jnp.float32),
        lax.psum(shares[6].astype(jnp.bfloat16), "dp").astype(jnp.float32),
        lax.psum(shares[7].astype(jnp.bfloat16), "dp").astype(jnp.float32),
        lax.psum(shares[8].astype(jnp.bfloat16), "dp").astype(jnp.float32),
        lax.psum(shares[9].astype(jnp.bfloat16), "dp").astype(jnp.float32),
    )
    return (
        result,
        grad_hidden.astype(jnp.bfloat16),
        totals[0],
        totals[1],
        totals[2],
        totals[3],
        totals[4],
        totals[5],
        totals[6],
        totals[7],
        totals[8],
        totals[9],
    )


def solution(mesh):
    in_specs = (
        P(("dp", "fsdp"), None),
        P("fsdp", None),
        P("fsdp", None),
        P("fsdp", None),
        P("fsdp", None),
        P("fsdp", None),
        P("fsdp", None),
        P("fsdp", None),
        P("fsdp"),
        P("fsdp"),
        P("fsdp", None),
        P(("dp", "fsdp")),
        P(("dp", "fsdp")),
        P(("dp", "fsdp")),
        P(("dp", "fsdp")),
        P(("dp", "fsdp"), None),
    )
    out_specs = (
        P(("dp", "fsdp"), None),
        P(("dp", "fsdp"), None),
        P("fsdp", None),
        P("fsdp", None),
        P("fsdp", None),
        P("fsdp", None),
        P("fsdp", None),
        P("fsdp", None),
        P("fsdp", None),
        P("fsdp"),
        P("fsdp"),
        P("fsdp", None),
    )
    return jax.shard_map(body, mesh=mesh, in_specs=in_specs, out_specs=out_specs, check_vma=False)
```

profile of v0, /device:TPU:0, one launch (start us, length us, event | category | flops | bytes accessed | tf_op | source)
XLA Modules:
  0.0 1400.7 jit_solution(12007780862260057249)
XLA Ops:
  19.1 7.1 gather_fusion.3
  31.9 14.3 %all-gather = bf16[4,240,3]{1,2,0:T(4,128)(2,1)S(1)} all-gather(bf16[1,240,3]{1,2,0:T(4,128)(2,1)S(1)} %bitcast.678), channel_id=1, replica_groups=mesh['dp'=8,'fsdp'=4] {'fsdp'}, dimensions={0}, use_global_device_ids=true | all-gather | bytes 7200 | tf_op jit(solution)/shard_map/all_gather | solution.py:268
  50.4 10.1 all-reduce.20
  60.6 21.1 %all-gather.1 = bf16[4,240,320]{1,2,0:T(8,128)(2,1)S(1)} all-gather(bf16[1,240,320]{1,2,0:T(8,128)(2,1)S(1)} %bitcast.667), channel_id=1, replica_groups=mesh['dp'=8,'fsdp'=4] {'fsdp'}, dimensions={0}, use_global_device_ids=true | all-gather | bytes 768000 | tf_op jit(solution)/shard_map/all_gather | solution.py:260
  85.6 25.1 %all-gather.2 = bf16[4,240,320]{1,2,0:T(8,128)(2,1)S(1)} all-gather(bf16[1,240,320]{1,2,0:T(8,128)(2,1)S(1)} %bitcast.668), channel_id=1, replica_groups=mesh['dp'=8,'fsdp'=4] {'fsdp'}, dimensions={0}, use_global_device_ids=true | all-gather | bytes 768000 | tf_op jit(solution)/shard_map/all_gather | solution.py:261
  149.5 44.6 %while.99 = (s32[]{:T(128)}, bf16[5,3,768,64]{2,3,1,0:T(8,128)(2,1)}, f32[5,3,768,1]{2,1,3,0:T(4,128)}, f32[5,3,768,1]{2,1,3,0:T(4,128)}, bf16[5,3,768,64]{2,3,1...) while((s32[]{:T(128)}, ...), condition=%wide.region_4.6_spmd.clone.clone, body=%wide.region_1.5_spmd.clone.sunk.clone | while | flops 475983360 | bytes 24771688 | solution.py:85
  194.2 5.7 multiply_reduce_fusion.8
  202.9 6.4 all-gather.13.cloned.1.call-done
  209.3 10.5 fusion.219
  219.8 82.0 %all-gather.15.cloned.1.call-done = bf16[960,2560]{1,0:T(8,128)(2,1)} async-done(((bf16[240,2560]{1,0:T(8,128)(2,1)}), bf16[960,2560]{1,0:T(8,128)(2,1)}) %all-gather.15.cloned.1.call-update) | async-done | bytes 4915216 | tf_op jit(solution)/shard_map/all_gather | solution.py:264
  301.8 14.8 %multiply_convert_fusion.5 = (bf16[768,2560]{1,0:T(8,128)(2,1)}, f32[768,2560]{1,0:T(8,128)}) fusion(f32[768,2560]{1,0:T(8,128)} %fusion.219, bf16[768,960]{0,1:T(8,128)(2,1)} %multiply_convert_fusion.9, bf16[960,2560]{1,0:T(8,128)(2,1)} %all-gather.15.cloned.1.call-done), kind=kOutput, calls=%fused_computation.204 | convolution fusion | flops 3786670080 | bytes 26050560 | tf_op jit(solution)/shard_map/kd,df->kf/dot_general | solution.py:20
  316.6 77.7 %all-gather.17.cloned.1.call-done = bf16[2560,960]{0,1:T(8,128)(2,1)} async-done(((bf16[640,960]{0,1:T(8,128)(2,1)}), bf16[2560,960]{0,1:T(8,128)(2,1)}) %all-gather.17.cloned.1.call-update) | async-done | bytes 4915216 | tf_op jit(solution)/shard_map/all_gather | solution.py:265
  394.2 11.2 multiply_add_fusion
  407.8 9.7 scatter_fusion
  417.5 5.8 gather_fusion.4
  432.5 29.0 %while.100 = (s32[]{:T(128)}, bf16[5,3,512,64]{2,3,1,0:T(8,128)(2,1)}, f32[5,3,512,1]{2,1,3,0:T(4,128)}, f32[5,3,512,1]{2,1,3,0:T(4,128)}, bf16[5,3,512,64]{2,3,...) while((s32[]{:T(128)}, ...), condition=%wide.region_11.14_spmd.clone.clone, body=%wide.region_8.13_spmd.clone.sunk.clone | while | flops 211547136 | bytes 11272297 | solution.py:85
  482.6 7.4 scatter_fusion.1
  500.7 15.7 %while.101 = (s32[]{:T(128)}, bf16[5,3,256,64]{2,3,1,0:T(8,128)(2,1)S(1)}, f32[5,3,256,1]{2,1,3,0:T(4,128)}, f32[5,3,256,1]{2,1,3,0:T(4,128)}, bf16[5,3,256,64]{...) while((s32[]{:T(128)}, ...), condition=%wide.region_18.22_spmd.clone.clone, body=%wide.region_15.21_spmd.clone.sunk.clone | while | flops 52099584 | bytes 2886761 | solution.py:85
  537.3 39.8 %while.102 = (s32[]{:T(128)}, f32[5,3,256,64]{2,3,1,0:T(8,128)}, f32[5,256,64]{1,2,0:T(8,128)}, bf16[5,256,64]{1,2,0:T(8,128)(2,1)}, bf16[5,3,256,64]{2,3,1,0:T(...) while((s32[]{:T(128)}, f32[5,3,256,64]{2,3,1,0:T(8,128)}, ...), condition=%wide.region_25.29_spmd.clone.clone, body=%wide.region_23.28_spmd.clone.sunk.clone | while | flops 128056576 | bytes 6882433 | solution.py:111
  596.8 6.0 gather_fusion.7
  604.7 9.5 multiply_convert_fusion.6
  614.2 6.6 fusion.226
  620.8 6.1 multiply_reduce_fusion.10
  631.4 59.6 %while.103 = (s32[]{:T(128)}, f32[5,3,512,64]{2,3,1,0:T(8,128)}, f32[5,512,64]{1,2,0:T(8,128)}, bf16[5,512,64]{1,2,0:T(8,128)(2,1)}, bf16[5,3,512,64]{2,3,1,0:T(...) while((s32[]{:T(128)}, f32[5,3,512,64]{2,3,1,0:T(8,128)}, ...), condition=%wide.region_32.36_spmd.clone.clone, body=%wide.region_30.35_spmd.clone.sunk.clone | while | flops 512096768 | bytes 25814144 | solution.py:111
  705.6 6.4 scatter_fusion.4
  712.0 7.0 gather_fusion.8
  721.4 12.9 multiply_convert_fusion.3
  734.4 7.9 fusion.228
  742.3 7.4 multiply_reduce_fusion.3
  754.1 94.3 %while.104 = (s32[]{:T(128)}, f32[5,3,768,64]{2,3,1,0:T(8,128)}, f32[5,768,64]{1,2,0:T(8,128)}, bf16[5,768,64]{1,2,0:T(8,128)(2,1)}, bf16[5,3,768,64]{2,3,1,0:T(...) while((s32[]{:T(128)}, f32[5,3,768,64]{2,3,1,0:T(8,128)}, ...), condition=%wide.region_39.43_spmd.clone.clone, body=%wide.region_37.42_spmd.clone.sunk.clone | while | flops 1152120576 | bytes 85118104 | solution.py:111
  857.2 10.8 fusion.190
  873.2 7.9 add_convert_fusion
  881.1 7.9 copy.128
  909.4 6.5 fusion.239
  915.9 8.1 add_convert_fusion.2
  928.8 6.5 fusion.241
  935.3 8.0 add_convert_fusion.1
  965.5 29.1 %reduce-scatter.29.cloned.1.call-done = bf16[640,960]{1,0:T(8,128)(2,1)} async-done(((bf16[2560,960]{1,0:T(8,128)(2,1)}), bf16[640,960]{1,0:T(8,128)(2,1)}) %reduce-scatter.29.cloned.1.call-update) | async-done | bytes 1228816
  997.0 42.6 %reduce-scatter.17.cloned.1.call-done = bf16[240,960]{1,0:T(8,128)(2,1)} async-done(((bf16[960,960]{1,0:T(8,128)(2,1)}), bf16[240,960]{1,0:T(8,128)(2,1)}) %reduce-scatter.17.cloned.1.call-update) | async-done | bytes 460816 | tf_op jit(solution)/shard_map/reduce_scatter | solution.py:289
  1039.7 43.5 %reduce-scatter.19.cloned.1.call-done = bf16[240,960]{1,0:T(8,128)(2,1)} async-done(((bf16[960,960]{1,0:T(8,128)(2,1)}), bf16[240,960]{1,0:T(8,128)(2,1)}) %reduce-scatter.19.cloned.1.call-update) | async-done | bytes 460816 | tf_op jit(solution)/shard_map/reduce_scatter | solution.py:298
  1083.1 90.0 %reduce-scatter.21.cloned.1.call-done = bf16[240,2560]{1,0:T(8,128)(2,1)} async-done(((bf16[960,2560]{1,0:T(8,128)(2,1)}), bf16[240,2560]{1,0:T(8,128)(2,1)}) %reduce-scatter.21.cloned.1.call-update) | async-done | bytes 1228816 | tf_op jit(solution)/shard_map/reduce_scatter | solution.py:301
  1173.1 91.2 %reduce-scatter.23.cloned.1.call-done = bf16[240,2560]{1,0:T(8,128)(2,1)} async-done(((bf16[960,2560]{1,0:T(8,128)(2,1)}), bf16[240,2560]{1,0:T(8,128)(2,1)}) %reduce-scatter.23.cloned.1.call-update) | async-done | bytes 1228816 | tf_op jit(solution)/shard_map/reduce_scatter | solution.py:304
  1267.5 6.5 scatter_fusion.2
  1281.9 6.5 fusion.156
  1290.8 9.7 scatter_fusion.5
  1305.5 11.0 all-reduce.19
  1317.5 11.9 all-reduce.17
  1331.2 50.0 %all-reduce.23.cloned.1.call-done = (bf16[240,960]{1,0:T(8,128)(2,1)}, bf16[240,320]{0,1:T(8,128)(2,1)}, bf16[240,320]{0,1:T(8,128)(2,1)}, bf16[240,960]{1,0:T(8...) async-done(((bf16[240,960]{1,0:T(8,128)(2,1)}, bf16[240,320]{0,1:T(8,128)(2,1)}, bf16[240,320]{0,1:T(8,128)(2,1)}, ...) | async-done | bytes 4915216 | tf_op jit(solution)/shard_map/psum | solution.py:361
  (875 shorter events, 554.1 us)
Async XLA Ops:
  7.2 21.4 %copy-start = (s32[1024]{0:T(1024)S(1)}, s32[1024]{0:T(1024)}, u32[]{:S(2)}) copy-start(s32[1024]{0:T(1024)} %param.51) | copy-start | bytes 12292
  7.2 136.7 %all-gather.9.cloned.1.call-start = ((), (), s32[]{:S(2)}) async-start(), calls=%async_computation.8 | async-start | bytes 2457600 | tf_op jit(solution)/shard_map/all_gather | solution.py:259
  7.9 186.2 %all-gather.11.cloned.1.call-start = ((), (), s32[]{:S(2)}) async-start(), calls=%async_computation.9 | async-start | bytes 2457600 | tf_op jit(solution)/shard_map/all_gather | solution.py:262
  8.7 200.6 %all-gather.13.cloned.1.call-start = ((), (), s32[]{:S(2)}) async-start(), calls=%async_computation.10 | async-start | bytes 6144000 | tf_op jit(solution)/shard_map/all_gather | solution.py:263
  9.4 292.4 %all-gather.15.cloned.1.call-start = ((), (), s32[]{:S(2)}) async-start(), calls=%async_computation.11 | async-start | bytes 6144000 | tf_op jit(solution)/shard_map/all_gather | solution.py:264
  10.0 384.2 %all-gather.17.cloned.1.call-start = ((), (), s32[]{:S(2)}) async-start(), calls=%async_computation.12 | async-start | bytes 6144000 | tf_op jit(solution)/shard_map/all_gather | solution.py:265
  10.6 951.5 %reduce-scatter.25.cloned.1.call-start = ((), (), s32[]{:S(2)}) async-start(), calls=%async_computation.17 | async-start | bytes 921600
  19.1 388.7 %copy-start.131 = (s32[768]{0:T(1024)}, s32[768]{0:T(1024)S(1)}, u32[]{:S(2)}) copy-start(s32[768]{0:T(1024)S(1)} %compare_select_fusion) | copy-start | bytes 9220
  28.6 365.6 %copy-start.3 = (f32[768,960]{0,1:T(8,128)}, f32[768,960]{0,1:T(8,128)S(1)}, u32[]{:S(2)}) copy-start(f32[768,960]{0,1:T(8,128)S(1)} %copy.94) | copy-start | bytes 8847364
  31.8 362.4 %copy-start.121 = (pred[768]{0:T(1024)(128)(4,1)}, pred[768]{0:T(1024)(128)(4,1)S(1)}, u32[]{:S(2)}) copy-start(pred[768]{0:T(1024)(128)(4,1)S(1)} %get-tuple-element.736) | copy-start | bytes 2308
  46.3 14.2 %copy-start.119 = (bf16[240,320]{0,1:T(8,128)(2,1)S(1)}, bf16[240,320]{0,1:T(8,128)(2,1)}, u32[]{:S(2)}) copy-start(bf16[240,320]{0,1:T(8,128)(2,1)} %param.42) | copy-start | bytes 460804
  46.7 38.9 %copy-start.141 = (f32[768]{0:T(1024)}, f32[768]{0:T(1024)S(1)}, u32[]{:S(2)}) copy-start(f32[768]{0:T(1024)S(1)} %multiply_reduce_fusion.9) | copy-start | bytes 9220
  46.7 38.9 %copy-start.120 = (bf16[240,320]{0,1:T(8,128)(2,1)S(1)}, bf16[240,320]{0,1:T(8,128)(2,1)}, u32[]{:S(2)}) copy-start(bf16[240,320]{0,1:T(8,128)(2,1)} %param.43) | copy-start | bytes 460804
  47.9 12.6 copy-start.143
  48.5 345.7 %copy-start.173 = (f32[768]{0:T(1024)}, f32[768]{0:T(1024)S(1)}, u32[]{:S(2)}) copy-start(f32[768]{0:T(1024)S(1)} %add_divide_fusion.3) | copy-start | bytes 9220
  60.5 640.6 %copy-start.115 = (f32[960]{0:T(1024)}, f32[960]{0:T(1024)S(1)}, u32[]{:S(2)}) copy-start(f32[960]{0:T(1024)S(1)} %convert_element_type.370) | copy-start | bytes 11524
  60.5 54.1 %copy-start.126 = (f32[768]{0:T(1024)}, f32[768]{0:T(1024)S(1)}, u32[]{:S(2)}) copy-start(f32[768]{0:T(1024)S(1)} %fusion.195) | copy-start | bytes 9220
  118.8 630.9 %copy-start.117 = (f32[960]{0:T(1024)}, f32[960]{0:T(1024)S(1)}, u32[]{:S(2)}) copy-start(f32[960]{0:T(1024)S(1)} %convert_element_type.378) | copy-start | bytes 11524
  119.4 298.1 %copy-start.154 = (s32[1024]{0:T(1024)}, s32[1024]{0:T(1024)S(1)}, u32[]{:S(2)}) copy-start(s32[1024]{0:T(1024)S(1)} %pad_clamp_fusion.1) | copy-start | bytes 12292
  121.7 579.4 %copy-start.124 = (pred[512]{0:T(512)(128)(4,1)}, pred[512]{0:T(512)(128)(4,1)S(1)}, u32[]{:S(2)}) copy-start(pred[512]{0:T(512)(128)(4,1)S(1)} %get-tuple-element.731) | copy-start | bytes 1540
  122.2 25.6 %copy-start.65 = (f32[768,32]{0,1:T(8,128)}, f32[768,32]{0,1:T(8,128)S(1)}, u32[]{:S(2)}) copy-start(f32[768,32]{0,1:T(8,128)S(1)} %get-tuple-element.793) | copy-start | bytes 294916
  122.2 25.6 %copy-start.67 = (f32[768,32]{0,1:T(8,128)}, f32[768,32]{0,1:T(8,128)S(1)}, u32[]{:S(2)}) copy-start(f32[768,32]{0,1:T(8,128)S(1)} %get-tuple-element.794) | copy-start | bytes 294916
  122.5 308.1 %copy-start.83 = (f32[512,32]{0,1:T(8,128)}, f32[512,32]{0,1:T(8,128)S(1)}, u32[]{:S(2)}) copy-start(f32[512,32]{0,1:T(8,128)S(1)} %get-tuple-element.795) | copy-start | bytes 196612
  122.5 308.1 %copy-start.85 = (f32[512,32]{0,1:T(8,128)}, f32[512,32]{0,1:T(8,128)S(1)}, u32[]{:S(2)}) copy-start(f32[512,32]{0,1:T(8,128)S(1)} %get-tuple-element.796) | copy-start | bytes 196612
  199.8 20.0 %copy-start.145 = (f32[768]{0:T(1024)}, f32[768]{0:T(1024)S(1)}, u32[]{:S(2)}) copy-start(f32[768]{0:T(1024)S(1)} %get-tuple-element.732) | copy-start | bytes 9220
  199.8 20.0 %copy-start.128 = (f32[768]{0:T(1024)}, f32[768]{0:T(1024)S(1)}, u32[]{:S(2)}) copy-start(f32[768]{0:T(1024)S(1)} %fusion.196) | copy-start | bytes 9220
  425.2 49.7 %copy-start.5 = (f32[512,960]{0,1:T(8,128)}, f32[512,960]{0,1:T(8,128)S(1)}, u32[]{:S(2)}) copy-start(f32[512,960]{0,1:T(8,128)S(1)} %copy.99) | copy-start | bytes 5898244
  429.0 197.9 %copy-start.137 = (f32[512]{0:T(512)}, f32[512]{0:T(512)S(1)}, u32[]{:S(2)}) copy-start(f32[512]{0:T(512)S(1)} %add_divide_fusion.4) | copy-start | bytes 6148
  496.4 91.7 %copy-start.8 = (f32[256,960]{0,1:T(8,128)}, f32[256,960]{0,1:T(8,128)S(1)}, u32[]{:S(2)}) copy-start(f32[256,960]{0,1:T(8,128)S(1)} %copy.101) | copy-start | bytes 2949124
  520.1 13.9 copy-start.41
  520.1 13.9 copy-start.166
  520.1 67.9 %copy-start.152 = (f32[256]{0:T(256)}, f32[256]{0:T(256)S(1)}, u32[]{:S(2)}) copy-start(f32[256]{0:T(256)S(1)} %get-tuple-element.818) | copy-start | bytes 3076
  604.7 96.5 %copy-start.12 = (f32[512,960]{0,1:T(8,128)}, f32[512,960]{0,1:T(8,128)S(1)}, u32[]{:S(2)}) copy-start(f32[512,960]{0,1:T(8,128)S(1)} %copy.106) | copy-start | bytes 5898244
  631.4 59.7 %copy-start.84 = (f32[512,32]{0,1:T(8,128)S(1)}, f32[512,32]{0,1:T(8,128)}, u32[]{:S(2)}) copy-start(f32[512,32]{0,1:T(8,128)} %copy-done.83) | copy-start | bytes 196612
  631.4 59.7 %copy-start.86 = (f32[512,32]{0,1:T(8,128)S(1)}, f32[512,32]{0,1:T(8,128)}, u32[]{:S(2)}) copy-start(f32[512,32]{0,1:T(8,128)} %copy-done.85) | copy-start | bytes 196612
  721.4 28.4 %copy-start.14 = (f32[768,960]{0,1:T(8,128)}, f32[768,960]{0,1:T(8,128)S(1)}, u32[]{:S(2)}) copy-start(f32[768,960]{0,1:T(8,128)S(1)} %copy.108) | copy-start | bytes 8847364
  754.1 94.3 %copy-start.66 = (f32[768,32]{0,1:T(8,128)S(1)}, f32[768,32]{0,1:T(8,128)}, u32[]{:S(2)}) copy-start(f32[768,32]{0,1:T(8,128)} %copy-done.65) | copy-start | bytes 294916
  754.1 94.3 %copy-start.68 = (f32[768,32]{0,1:T(8,128)S(1)}, f32[768,32]{0,1:T(8,128)}, u32[]{:S(2)}) copy-start(f32[768,32]{0,1:T(8,128)} %copy-done.67) | copy-start | bytes 294916
  853.2 110.6 %reduce-scatter.27.cloned.1.call-start = ((), (), s32[]{:S(2)}) async-start(), calls=%async_computation.18 | async-start | bytes 921600
  857.2 11.3 copy-start.138
  868.1 126.6 %reduce-scatter.29.cloned.1.call-start = ((), (), s32[]{:S(2)}) async-start(), calls=%async_computation.19 | async-start | bytes 6553600
  889.0 150.6 %reduce-scatter.17.cloned.1.call-start = ((), (), s32[]{:S(2)}) async-start(), calls=%async_computation.13 | async-start | bytes 2457600 | tf_op jit(solution)/shard_map/reduce_scatter | solution.py:289
  898.4 184.7 %reduce-scatter.19.cloned.1.call-start = ((), (), s32[]{:S(2)}) async-start(), calls=%async_computation.14 | async-start | bytes 2457600 | tf_op jit(solution)/shard_map/reduce_scatter | solution.py:298
  904.5 268.6 %reduce-scatter.21.cloned.1.call-start = ((), (), s32[]{:S(2)}) async-start(), calls=%async_computation.15 | async-start | bytes 6144000 | tf_op jit(solution)/shard_map/reduce_scatter | solution.py:301
  924.0 340.3 %reduce-scatter.23.cloned.1.call-start = ((), (), s32[]{:S(2)}) async-start(), calls=%async_computation.16 | async-start | bytes 6144000 | tf_op jit(solution)/shard_map/reduce_scatter | solution.py:304
  943.3 373.3 %reduce-scatter.31.cloned.1.call-start = ((), (), s32[]{:S(2)}) async-start(), calls=%async_computation.20 | async-start | bytes 307200
  962.0 419.2 %all-reduce.23.cloned.1.call-start = ((), (), s32[]{:S(2)}) async-start(), calls=%async_computation.21 | async-start | bytes 9994240 | tf_op jit(solution)/shard_map/psum | solution.py:361
  997.0 267.3 %copy-start.184 = (bf16[960]{0:T(1024)(128)(2,1)S(1)}, bf16[960]{0:T(1024)(128)(2,1)}, u32[]{:S(2)}) copy-start(bf16[960]{0:T(1024)(128)(2,1)} %get-tuple-element.576) | copy-start | bytes 5764
  (180 other events, 637.3 us)
Sparse Core Ops, SparseCore 0:
  9.6 46.4 all-gather.8
  57.6 58.0 all-gather.10
  117.3 91.9 all-gather.12
  210.7 91.0 all-gather.14
  303.2 91.0 all-gather.16
  853.3 21.4 reduce-scatter.24
  877.1 22.2 reduce-scatter.26
  901.7 92.9 reduce-scatter.28
  997.5 42.0 reduce-scatter.16
  1042.4 40.6 reduce-scatter.18
  1085.5 87.5 reduce-scatter.20
  1175.3 88.9 reduce-scatter.22
  1267.1 20.4 reduce-scatter.30
  1292.3 88.8 all-reduce.22
where the time goes:
time: 1410 us; the launch traced here: 1400 us
  waiting for transfers between devices  516 us (37%)
  matrix products  460 us (33%)
  local copies, waits for them, and re-layouts  194 us (14%)
  other arithmetic  116 us (8%)
  blocking collectives  93.6 us (7%)
  between operations  18.5 us (1%)
    dot_general x168, matrix products, low_dot(): return jnp.einsum(spec, left, right, preferred_element_type=jnp.float32)  453 us
    reduce_scatter x1, waiting for transfers between devices, reduce_end(): lax.psum_scatter(summed[5].astype(jnp.bfloat16), 'fsdp', scatter_dimensio...  91.2 us
    reduce_scatter x1, waiting for transfers between devices, reduce_end(): lax.psum_scatter(summed[4].astype(jnp.bfloat16), 'fsdp', scatter_dimensio...  90 us
    all_gather x1, waiting for transfers between devices, gather_forward(): lax.all_gather(shards[5], 'fsdp', axis=0, tiled=True)  82 us
    all_gather x1, waiting for transfers between devices, gather_forward(): lax.all_gather(shards[6], 'fsdp', axis=0, tiled=True)  77.7 us
    unnamed x440, local copies, waits for them, and re-layouts  56.7 us
    psum x1, waiting for transfers between devices, body(): lax.psum(shares[0].astype(jnp.bfloat16), 'dp').astype(jnp.float32)  50 us
    reduce_scatter x1, waiting for transfers between devices, reduce_end(): lax.psum_scatter(summed[3].astype(jnp.bfloat16), 'fsdp', scatter_dimensio...  43.5 us
  transfers between devices with their start and end apart: 14, of which 9 were waited for; matrix products, arithmetic and copies ran while one was open for 21% of the time, Pallas kernels for 0%

commit v1 on v0

v1 whole, which is shorter than its diff:
```python
import functools
import math

import jax
import jax.numpy as jnp
from jax import lax
from jax.experimental import pallas as pl
from jax.experimental.pallas import tpu as pltpu
from jax.sharding import PartitionSpec as P

HEADS = 15
KV_HEADS = 5
HEAD_DIM = 64
HALF = HEAD_DIM // 2
GROUP = HEADS // KV_HEADS
NREC = 3
ROWS = 256

norm_eps = 1e-05
masked_score = -1e30
highest = lax.Precision.HIGHEST
f32 = jnp.float32
bf16 = jnp.bfloat16


def dot(spec, left, right):
    return jnp.einsum(spec, left, right, preferred_element_type=f32)


def swap_halves(x):
    return jnp.concatenate([x[:, HALF:], x[:, :HALF]], axis=1)


def matmul(a, b, dims):
    return lax.dot_general(a, b, (dims, ((), ())), preferred_element_type=f32)


QW = HEADS * HEAD_DIM
KW = KV_HEADS * HEAD_DIM


def attend_fwd_kernel(qkv_ref, cos_ref, sin_ref, cols_ref, rows_ref, o_ref, q_ref, k_ref, v_ref, lse_ref, bias, stats):
    step = pl.program_id(0)
    rows = pl.ds(pl.multiple_of(step * ROWS, ROWS), ROWS)

    @pl.when(step == 0)
    def _():
        cos, sin = cos_ref[...], sin_ref[...]
        for g in range(KV_HEADS):
            raw = qkv_ref[:, QW + g * HEAD_DIM : QW + (g + 1) * HEAD_DIM]
            k_ref[g] = (raw * cos + swap_halves(raw) * sin).astype(bf16)
            v_ref[g] = qkv_ref[:, QW + KW + g * HEAD_DIM : QW + KW + (g + 1) * HEAD_DIM].astype(bf16)

    cols = cols_ref[rows, :]
    token, begin = cols[:, 0:1], cols[:, 1:2]
    key_token = rows_ref[0:1, :]
    bias[...] = jnp.where((key_token <= token) & (key_token >= begin), 0.0, masked_score)
    cos, sin = cos_ref[rows, :], sin_ref[rows, :]
    stats[...] = jnp.zeros_like(stats)
    for n in range(HEADS):
        g = n // GROUP
        raw = qkv_ref[rows, n * HEAD_DIM : (n + 1) * HEAD_DIM]
        q = ((raw * cos + swap_halves(raw) * sin).astype(bf16).astype(f32) * (1.0 / math.sqrt(HEAD_DIM))).astype(bf16)
        q_ref[n, rows, :] = q
        s = matmul(q, k_ref[g], ((1,), (1,))) + bias[...]
        m = jnp.max(s, axis=1, keepdims=True)
        p = jnp.exp(s - m)
        t = jnp.sum(p, axis=1, keepdims=True)
        p = (p * (1.0 / t)).astype(bf16)
        o_ref[rows, n * HEAD_DIM : (n + 1) * HEAD_DIM] = matmul(p, v_ref[g], ((1,), (0,))).astype(bf16)
        stats[:, n : n + 1] = m + jnp.log(t)
    lse_ref[...] = jnp.transpose(stats[...])[:16]


def attend_fwd(qkv, cos, sin, cols, rows):
    k = qkv.shape[0]
    whole = lambda *shape: pl.BlockSpec(shape, lambda i: (0,) * len(shape))
    return pl.pallas_call(
        attend_fwd_kernel,
        grid=(k // ROWS,),
        out_shape=(
            jax.ShapeDtypeStruct((k, QW), bf16),
            jax.ShapeDtypeStruct((HEADS, k, HEAD_DIM), bf16),
            jax.ShapeDtypeStruct((KV_HEADS, k, HEAD_DIM), bf16),
            jax.ShapeDtypeStruct((KV_HEADS, k, HEAD_DIM), bf16),
            jax.ShapeDtypeStruct((16, k), f32),
        ),
        in_specs=[
            whole(k, QW + 2 * KW),
            whole(k, HEAD_DIM),
            whole(k, HEAD_DIM),
            whole(k, 2),
            whole(2, k),
        ],
        out_specs=(
            whole(k, QW),
            whole(HEADS, k, HEAD_DIM),
            whole(KV_HEADS, k, HEAD_DIM),
            whole(KV_HEADS, k, HEAD_DIM),
            pl.BlockSpec((16, ROWS), lambda i: (0, i)),
        ),
        scratch_shapes=[pltpu.VMEM((ROWS, k), f32), pltpu.VMEM((ROWS, 128), f32)],
        compiler_params=pltpu.CompilerParams(vmem_limit_bytes=56 << 20),
        name="attend_fwd",
    )(qkv, cos, sin, cols, rows)


def attend_bwd_kernel(
    q_ref, k_ref, v_ref, lse_ref, do_ref, cos_ref, sin_ref, cols_ref, rows_ref, out_ref, bias, dk, dv, kt
):
    step = pl.program_id(0)
    start = pl.multiple_of(step * ROWS, ROWS)
    rows = pl.ds(start, ROWS)

    @pl.when(step == 0)
    def _():
        dk[...] = jnp.zeros_like(dk)
        dv[...] = jnp.zeros_like(dv)
        for g in range(KV_HEADS):
            kt[g] = jnp.transpose(k_ref[g].astype(f32)).astype(bf16)

    key_token = cols_ref[:, 0:1]
    token, begin = rows_ref[0:1, pl.ds(start, ROWS)], rows_ref[1:2, pl.ds(start, ROWS)]
    bias[...] = jnp.where((key_token <= token) & (key_token >= begin), 0.0, masked_score)
    cos, sin = cos_ref[rows, :], sin_ref[rows, :]
    for n in range(HEADS):
        g = n // GROUP
        q = q_ref[n, rows, :]
        do = do_ref[rows, n * HEAD_DIM : (n + 1) * HEAD_DIM]
        s = matmul(k_ref[g], q, ((1,), (1,))) + bias[...]
        p = jnp.exp(s - lse_ref[n : n + 1, :])
        dp = matmul(v_ref[g], do, ((1,), (1,)))
        dv[g] += matmul(p.astype(bf16), do, ((1,), (0,)))
        pd = p * dp
        ds = (pd - p * jnp.sum(pd, axis=0, keepdims=True)).astype(bf16)
        dk[g] += matmul(ds, q, ((1,), (0,)))
        dq = jnp.transpose(matmul(kt[g], ds, ((1,), (0,)))) * (1.0 / math.sqrt(HEAD_DIM))
        out_ref[rows, n * HEAD_DIM : (n + 1) * HEAD_DIM] = (dq * cos - swap_halves(dq) * sin).astype(bf16)

    @pl.when(step == pl.num_programs(0) - 1)
    def _():
        cos, sin = cos_ref[...], sin_ref[...]
        for g in range(KV_HEADS):
            grad = dk[g]
            out_ref[:, QW + g * HEAD_DIM : QW + (g + 1) * HEAD_DIM] = (
                grad * cos - swap_halves(grad) * sin
            ).astype(bf16)
            out_ref[:, QW + KW + g * HEAD_DIM : QW + KW + (g + 1) * HEAD_DIM] = dv[g].astype(bf16)


def attend_bwd(q, k, v, lse, grad, cos, sin, cols, rows):
    count = grad.shape[0]
    whole = lambda *shape: pl.BlockSpec(shape, lambda i: (0,) * len(shape))
    return pl.pallas_call(
        attend_bwd_kernel,
        grid=(count // ROWS,),
        out_shape=jax.ShapeDtypeStruct((count, QW + 2 * KW), bf16),
        in_specs=[
            whole(HEADS, count, HEAD_DIM),
            whole(KV_HEADS, count, HEAD_DIM),
            whole(KV_HEADS, count, HEAD_DIM),
            pl.BlockSpec((16, ROWS), lambda i: (0, i)),
            whole(count, QW),
            whole(count, HEAD_DIM),
            whole(count, HEAD_DIM),
            whole(count, 2),
            whole(2, count),
        ],
        out_specs=whole(count, QW + 2 * KW),
        scratch_shapes=[
            pltpu.VMEM((count, ROWS), f32),
            pltpu.VMEM((KV_HEADS, count, HEAD_DIM), f32),
            pltpu.VMEM((KV_HEADS, count, HEAD_DIM), f32),
            pltpu.VMEM((KV_HEADS, HEAD_DIM, count), bf16),
        ],
        compiler_params=pltpu.CompilerParams(vmem_limit_bytes=56 << 20),
        name="attend_bwd",
    )(q, k, v, lse, grad, cos, sin, cols, rows)


def inverse_rms(values):
    return lax.rsqrt(jnp.mean(values * values, axis=-1, keepdims=True) + norm_eps)


def norm_back(values, gain, grad):
    scale = inverse_rms(values)
    unit = values * scale
    grad_unit = grad * gain
    grad_values = (grad_unit - unit * jnp.mean(grad_unit * unit, axis=-1, keepdims=True)) * scale
    return grad_values, jnp.sum(grad * unit, axis=0)


def forward_step(rows_in, tables, weights, section):
    wqkv, wo, wg, wu, wd, gain_attn, gain_ffn, router = weights
    normed = (rows_in * inverse_rms(rows_in) * gain_attn).astype(bf16)
    qkv = dot("kd,de->ke", normed, wqkv)
    mixed, q, k, v, lse = attend_fwd(qkv, *tables)
    attn = dot("ke,ed->kd", mixed, wo)
    middle = rows_in + attn
    inner = (middle * inverse_rms(middle) * gain_ffn).astype(bf16)
    gate = dot("kd,df->kf", inner, wg)
    up = dot("kd,df->kf", inner, wu)
    activated = (gate * jax.nn.sigmoid(gate) * up).astype(bf16)
    ffn = dot("kf,fd->kd", activated, wd)
    gate_c = jax.nn.sigmoid(jnp.sum(rows_in * router[:, section][None, :], axis=1, keepdims=True))
    branches = attn + ffn
    out = rows_in + gate_c * branches
    kept = (rows_in, normed, q, k, v, lse, mixed, middle, inner, gate.astype(bf16), up.astype(bf16), activated, gate_c, branches)
    return out, kept


def backward_step(grad_new, kept, tables, weights, section):
    wqkv, wo, wg, wu, wd, gain_attn, gain_ffn, router = weights
    rows_in, normed, q, k, v, lse, mixed, middle, inner, gate, up, activated, gate_c, branches = kept
    gate, up = gate.astype(f32), up.astype(f32)
    dz = jnp.sum(grad_new * branches, axis=1, keepdims=True) * gate_c * (1.0 - gate_c)
    router_grad = jnp.sum(rows_in * dz, axis=0)
    grad_rows = grad_new + dz * router[:, section][None, :]
    grad_branch = gate_c * grad_new
    grad_ffn = grad_branch.astype(bf16)
    grad_act = dot("kd,fd->kf", grad_ffn, wd)
    sig = jax.nn.sigmoid(gate)
    grad_gate = (grad_act * up * (sig + gate * sig * (1.0 - sig))).astype(bf16)
    grad_up = (grad_act * (gate * sig)).astype(bf16)
    grad_inner = dot("kf,df->kd", grad_gate, wg) + dot("kf,df->kd", grad_up, wu)
    grad_middle, gain_ffn_grad = norm_back(middle, gain_ffn, grad_inner)
    grad_attn = (grad_branch + grad_middle).astype(bf16)
    grad_mixed = dot("kd,ed->ke", grad_attn, wo).astype(bf16)
    grad_qkv = attend_bwd(q, k, v, lse, grad_mixed, *tables)
    grad_normed = dot("ke,de->kd", grad_qkv, wqkv)
    grad_norm_rows, gain_attn_grad = norm_back(rows_in, gain_attn, grad_normed)
    grad_rows = grad_rows + grad_middle + grad_norm_rows
    pairs = ((activated, grad_ffn), (inner, grad_gate), (inner, grad_up), (mixed, grad_attn), (normed, grad_qkv))
    return grad_rows, pairs, (gain_attn_grad, gain_ffn_grad, router_grad)


def gather_all(shard):
    if shard.shape[0] % lax.axis_size("dp"):
        return lax.all_gather(shard, "fsdp", axis=0, tiled=True)
    rows = shard.shape[0] // lax.axis_size("dp")
    part = lax.dynamic_slice_in_dim(shard, lax.axis_index("dp") * rows, rows, 0)
    return lax.all_gather(part, ("fsdp", "dp"), axis=0, tiled=True)


def reduce_all(total):
    chunks = lax.axis_size("dp") * lax.axis_size("fsdp")
    if total.shape[0] % chunks:
        part = lax.psum_scatter(total, "fsdp", scatter_dimension=0, tiled=True)
        return lax.psum(part, "dp")
    rows = total.shape[0] // chunks
    padded = jnp.pad(total.reshape(chunks, rows, -1), ((0, 0), (0, -rows % 16), (0, 0)))
    part = lax.psum_scatter(padded.reshape(-1, total.shape[1]), ("fsdp", "dp"), scatter_dimension=0, tiled=True)[:rows]
    return lax.all_gather(part, "dp", axis=0, tiled=True)


def body(
    inputs, w_query, w_key, w_value, w_out, w_gate, w_up, w_down, gain_attn, gain_ffn, w_router,
    seq_start, pick_first, pick_second, pick_third, out_grad,
):
    picks = (pick_first, pick_second, pick_third)
    counts = tuple(p.shape[0] for p in picks)
    tokens = inputs.shape[0]

    gathered1 = gather_all(jnp.concatenate([w_out, w_query, w_key, w_value], axis=1))
    wg, wu, wd = gather_all(w_gate), gather_all(w_up), gather_all(w_down)
    wo, wqkv = gathered1[:, :QW], gathered1[:, QW:]
    small = jnp.concatenate([gain_attn[:, None], gain_ffn[:, None], w_router], axis=1)
    small = lax.all_gather(small, "fsdp", axis=0, tiled=True).astype(f32)
    weights = (wqkv, wo, wg, wu, wd, small[:, 0], small[:, 1], small[:, 2:5])

    places = jnp.arange(tokens, dtype=jnp.int32)
    level = jnp.full((tokens,), NREC, jnp.int32)
    for p in picks:
        level = level - jnp.any(p[:, None] == places[None, :], axis=0).astype(jnp.int32)
    kinds = level[None, :] == jnp.arange(NREC + 1, dtype=jnp.int32)[:, None]
    before = (places[:, None] < places[None, :]).astype(bf16)
    ahead = dot("ct,tu->cu", kinds.astype(bf16), before).astype(jnp.int32)
    bases = jnp.array([0, counts[2], counts[1], counts[0]], jnp.int32)
    position = jnp.sum(jnp.where(kinds, ahead + bases[:, None], 0), axis=0)
    chosen = position[None, :] == places[:, None]
    order = chosen.astype(bf16)
    token = jnp.sum(jnp.where(chosen, places[None, :], 0), axis=1)
    begin = jnp.sum(jnp.where(chosen, seq_start[None, :], 0), axis=1)
    frequency = jnp.exp(jnp.arange(HALF, dtype=f32) * (-2.0 * math.log(10000.0) / HEAD_DIM))
    angles = (token - begin).astype(f32)[:, None] * frequency[None, :]
    cos, sin = jnp.cos(angles), jnp.sin(angles)
    cos = jnp.concatenate([cos, cos], axis=1)
    sin = jnp.concatenate([-sin, sin], axis=1)
    rows2 = jnp.stack([token, begin]).astype(f32)
    cols2 = jnp.stack([token, begin], axis=1).astype(f32)
    tables = [(cos[:k], sin[:k], cols2[:k], rows2[:, :k]) for k in counts]

    hidden = dot("pt,td->pd", order, inputs)
    grads = dot("pt,td->pd", order, out_grad)

    kept, news, rows_in = [], [], hidden[: counts[0]]
    for r in range(NREC):
        new, saved = forward_step(rows_in, tables[r], weights, r)
        kept.append(saved)
        news.append(new)
        if r + 1 < NREC:
            rows_in = new[: counts[r + 1]]
    final = jnp.concatenate(
        [
            news[2].astype(bf16),
            news[1][counts[2] :].astype(bf16),
            news[0][counts[1] :].astype(bf16),
            hidden[counts[0] :].astype(bf16),
        ],
        axis=0,
    )
    result = dot("pt,pd->td", order, final).astype(bf16)

    grad_new = grads[: counts[2]]
    pairs, smalls = [], []
    for r in reversed(range(NREC)):
        grad_rows, step_pairs, step_small = backward_step(grad_new, kept[r], tables[r], weights, r)
        pairs.append(step_pairs)
        smalls.append(step_small)
        if r > 0:
            grad_new = jnp.concatenate([grad_rows, grads[counts[r] : counts[r - 1]]], axis=0)
    grad_final = jnp.concatenate([grad_rows.astype(bf16), grads[counts[0] :].astype(bf16)], axis=0)
    grad_inputs = dot("pt,pd->td", order, grad_final).astype(bf16)

    sums = []
    for i in range(5):
        left = jnp.concatenate([p[i][0] for p in pairs], axis=0)
        right = jnp.concatenate([p[i][1] for p in pairs], axis=0)
        sums.append(dot("kd,ke->de", left, right).astype(bf16))
    down, gate, up, out, qkv = sums
    down, gate, up = reduce_all(down), reduce_all(gate), reduce_all(up)
    first = reduce_all(jnp.concatenate([out, qkv], axis=1)).astype(f32)
    small = jnp.stack(
        [smalls[0][0] + smalls[1][0] + smalls[2][0], smalls[0][1] + smalls[1][1] + smalls[2][1]]
        + [s[2] for s in reversed(smalls)],
        axis=1,
    )
    small = lax.psum_scatter(small, "fsdp", scatter_dimension=0, tiled=True)
    small = lax.psum(small, "dp")
    return (
        result,
        grad_inputs,
        first[:, QW : 2 * QW],
        first[:, 2 * QW : 2 * QW + KW],
        first[:, 2 * QW + KW :],
        first[:, :QW],
        gate.astype(f32),
        up.astype(f32),
        down.astype(f32),
        small[:, 0],
        small[:, 1],
        small[:, 2:5],
    )


def solution(mesh):
    tok, row = P(("dp", "fsdp")), P("fsdp")
    in_specs = (tok,) + (row,) * 10 + (tok,) * 5
    out_specs = (tok, tok) + (row,) * 10
    return jax.shard_map(body, mesh=mesh, in_specs=in_specs, out_specs=out_specs, check_vma=False)
```

time: 1410 us -> 1180 us (0.84)
  matrix products: 460 us -> 213 us
  Pallas kernels: 0 us -> 137 us
  waiting for transfers between devices: 516 us -> 621 us
  other arithmetic: 116 us -> 26.6 us
  blocking collectives: 93.6 us -> 27.5 us
  local copies, waits for them, and re-layouts: 194 us -> 132 us
    dot_general x174 -> x40, matrix products: 460 us -> 213 us  [dot(): return jnp.einsum(spec, left, right, preferred_element_type=f32)]
    pallas_call x0 -> x6, Pallas kernels: none -> 137 us  [the longest x3 72.1 us: attend_fwd(): pl.pallas_call(attend_fwd_kernel, grid=(k // ROWS,), out_shape=(jax.Shape...]
    reduce_scatter x4, waiting for transfers between devices: 267 us -> 401 us  [reduce_all(): lax.psum_scatter(padded.reshape(-1, total.shape[1]), ('fsdp', 'dp'), scat...]
    gather x15 -> x0, local copies, waits for them, and re-layouts: 54.8 us -> none  [the longest x6 24.5 us: backward_step(): grad_new = jnp.take(grad_hidden, token_index, axis=0)]
    convert_element_type x55 -> x14, other arithmetic: 61 us -> 9.19 us  [the longest x1 5.58 us: body(): grad_rows.astype(bf16)]
    psum x1 -> x0, waiting for transfers between devices: 50 us -> none  [body(): lax.psum(shares[0].astype(jnp.bfloat16), 'dp').astype(jnp.float32)]
    all_gather x5 -> x8, waiting for transfers between devices: 166 us -> 214 us  [the longest x4 139 us: gather_all(): return lax.all_gather(part, ('fsdp', 'dp'), axis=0, tiled=True)]
    all_gather x3 -> x1, blocking collectives: 60.6 us -> 14.9 us  [body(): small = lax.all_gather(small, 'fsdp', axis=0, tiled=True).astype(f32)]
  transfers between devices with their start and end apart: 14 -> 13, of which waited for: 9 -> 12; matrix products, arithmetic and copies ran while one was open for 21% -> 20% of each run, Pallas kernels for 0% -> 6%
where the time goes in v1:
time: 1180 us; the launch traced here: 1170 us
  waiting for transfers between devices  621 us (53%)
  matrix products  213 us (18%)
  Pallas kernels  137 us (12%)
  local copies, waits for them, and re-layouts  132 us (11%)
  blocking collectives  27.5 us (2%)
  other arithmetic  26.6 us (2%)
  between operations  15.8 us (1%)
    reduce_scatter x4, waiting for transfers between devices, reduce_all(): lax.psum_scatter(padded.reshape(-1, total.shape[1]), ('fsdp', 'dp'), scat...  401 us
    dot_general x40, matrix products, dot(): return jnp.einsum(spec, left, right, preferred_element_type=f32)  213 us
    all_gather x4, waiting for transfers between devices, gather_all(): return lax.all_gather(part, ('fsdp', 'dp'), axis=0, tiled=True)  139 us
    all_gather x4, waiting for transfers between devices, reduce_all(): return lax.all_gather(part, 'dp', axis=0, tiled=True)  75.1 us
    pallas_call x3, Pallas kernels, attend_fwd(): pl.pallas_call(attend_fwd_kernel, grid=(k // ROWS,), out_shape=(jax.Shape...  72.1 us
    pallas_call x3, Pallas kernels, attend_bwd(): pl.pallas_call(attend_bwd_kernel, grid=(count // ROWS,), out_shape=jax.Sh...  65.1 us
    unnamed x247, local copies, waits for them, and re-layouts  58.4 us
  transfers between devices with their start and end apart: 13, of which 12 were waited for; matrix products, arithmetic and copies ran while one was open for 20% of the time, Pallas kernels for 6%

profile of v1, /device:TPU:0, one launch (start us, length us, event | category | flops | bytes accessed | tf_op | source)
XLA Modules:
  0.0 1173.0 jit_solution(13716629658034005417)
XLA Ops:
  25.4 14.9 %all-gather = bf16[4,240,5]{1,2,0:T(8,128)(2,1)S(1)} all-gather(bf16[1,240,5]{1,2,0:T(8,128)(2,1)S(1)} %maximum_bitcast_fusion), channel_id=1, replica_groups=mesh['dp'=8,'fsdp'=4] {'fsdp'}, dimensions={0}, use_global_device_ids=true | all-gather | bytes 12000 | tf_op jit(solution)/shard_map/all_gather | solution.py:268
  55.4 26.2 %all-gather.20.cloned.1.call-done = bf16[32,30,2560]{2,1,0:T(8,128)(2,1)} async-done(((bf16[1,30,2560]{2,1,0:T(8,128)(2,1)}), bf16[32,30,2560]{2,1,0:T(8,128)(2,1)}) %all-gather.20.cloned.1.call-update) | async-done | bytes 4915216 | tf_op jit(solution)/shard_map/all_gather | solution.py:242
  81.6 7.6 reshape.259
  89.2 7.2 fusion.108.qkv_ref
  96.4 35.2 %attend_fwd.3 = (bf16[768,960]{1,0:T(8,128)(2,1)}, bf16[15,768,64]{2,1,0:T(8,128)(2,1)}, bf16[5,768,64]{2,1,0:T(8,128)(2,1)}, bf16[5,768,64]{2,1,0:T(8,128)(2,1)}, f32[16,768]{1,0:T(8,128)}) custom-call(f32[768,1600]{1,0:T(8,128)} %fusion.108.qkv_ref, f32[768,64]{1,0:T(8,128)} %get-tuple-element.183.cos_ref, f32[768,64]{1,0:T(8,128)} %get-tuple-element.182.sin_ref, ...), custom_call_target="tpu_custom_call" | custom-call | tf_op jit(solution)/shard_map/attend_fwd/pallas_call | solution.py:78
  131.6 17.3 %all-gather.22.cloned.1.call-done = bf16[32,30,2560]{2,1,0:T(8,128)(2,1)} async-done(((bf16[1,30,2560]{2,1,0:T(8,128)(2,1)}), bf16[32,30,2560]{2,1,0:T(8,128)(2,1)}) %all-gather.22.cloned.1.call-update) | async-done | bytes 4915216 | tf_op jit(solution)/shard_map/all_gather | solution.py:242
  148.8 7.7 reshape.261
  156.5 59.6 %all-gather.24.cloned.1.call-done = bf16[32,30,2560]{2,1,0:T(8,128)(2,1)} async-done(((bf16[1,30,2560]{2,1,0:T(8,128)(2,1)}), bf16[32,30,2560]{2,1,0:T(8,128)(2,1)}) %all-gather.24.cloned.1.call-update) | async-done | bytes 4915216 | tf_op jit(solution)/shard_map/all_gather | solution.py:242
  216.1 7.5 reshape.263
  223.6 6.2 multiply_reduce_fusion.6
  239.3 8.1 multiply_convert_fusion.2
  247.4 35.8 %all-gather.16.cloned.1.call-done = bf16[2560,960]{1,0:T(8,128)(2,1)} async-done(((bf16[80,960]{1,0:T(8,128)(2,1)}), bf16[2560,960]{1,0:T(8,128)(2,1)}) %all-gather.16.cloned.1.call-update) | async-done | bytes 4915216 | tf_op jit(solution)/shard_map/all_gather | solution.py:242
  283.2 11.6 multiply_add_fusion
  299.5 25.2 %attend_fwd.4 = (bf16[512,960]{1,0:T(8,128)(2,1)}, bf16[15,512,64]{2,1,0:T(8,128)(2,1)}, bf16[5,512,64]{2,1,0:T(8,128)(2,1)}, bf16[5,512,64]{2,1,0:T(8,128)(2,1)}, f32[16,512]{1,0:T(8,128)}) custom-call(f32[512,1600]{1,0:T(8,128)} %fusion.106.qkv_ref, f32[512,64]{1,0:T(8,128)} %get-tuple-element.185.cos_ref, f32[512,64]{1,0:T(8,128)} %get-tuple-element.184.sin_ref, ...), custom_call_target="tpu_custom_call" | custom-call | tf_op jit(solution)/shard_map/attend_fwd/pallas_call | solution.py:78
  331.8 10.1 multiply_convert_fusion.5
  342.0 5.8 multiply_add_fusion.2
  350.9 11.8 %attend_fwd.5 = (bf16[256,960]{1,0:T(8,128)(2,1)}, bf16[15,256,64]{2,1,0:T(8,128)(2,1)}, bf16[5,256,64]{2,1,0:T(8,128)(2,1)}, bf16[5,256,64]{2,1,0:T(8,128)(2,1)}, f32[16,256]{1,0:T(8,128)}) custom-call(f32[256,1600]{1,0:T(8,128)} %fusion.104.qkv_ref, f32[256,64]{1,0:T(8,128)} %get-tuple-element.187.cos_ref, f32[256,64]{1,0:T(8,128)} %get-tuple-element.186.sin_ref, ...), custom_call_target="tpu_custom_call" | custom-call | tf_op jit(solution)/shard_map/attend_fwd/pallas_call | solution.py:78
  386.1 8.1 attend_bwd.3
  394.2 4.6 multiply_reduce_fusion.20
  401.4 10.6 multiply_convert_fusion.3
  412.0 5.4 fusion.145
  427.8 20.3 %attend_bwd.4 = bf16[512,1600]{1,0:T(8,128)(2,1)} custom-call(bf16[15,512,64]{2,1,0:T(8,128)(2,1)} %get-tuple-element.34.q_ref, bf16[5,512,64]{2,1,0:T(8,128)(2,1)} %get-tuple-element.35.k_ref, bf16[5,512,64]{2,1,0:T(8,128)(2,1)} %get-tuple-element.36.v_ref, f32[16,512]{1,0:T(8,128)} %get-tuple-element.37.lse_ref, bf16[512,960]{1,0:T(8,128)(2,1)} %copy.92.do_ref, ...), custom_call_target="tpu_custom_call" | custom-call | tf_op jit(solution)/shard_map/attend_bwd/pallas_call | solution.py:154
  448.1 4.9 multiply_reduce_fusion.11
  458.6 10.4 fusion.21
  469.1 11.0 multiply_convert_fusion
  484.3 8.3 multiply_reduce_fusion.1
  500.7 36.7 %attend_bwd.5 = bf16[768,1600]{1,0:T(8,128)(2,1)} custom-call(bf16[15,768,64]{2,1,0:T(8,128)(2,1)} %get-tuple-element.38.q_ref, bf16[5,768,64]{2,1,0:T(8,128)(2,1)} %get-tuple-element.39.k_ref, bf16[5,768,64]{2,1,0:T(8,128)(2,1)} %get-tuple-element.40.v_ref, f32[16,768]{1,0:T(8,128)} %get-tuple-element.41.lse_ref, bf16[768,960]{1,0:T(8,128)(2,1)} %copy.93.do_ref, ...), custom_call_target="tpu_custom_call" | custom-call | tf_op jit(solution)/shard_map/attend_bwd/pallas_call | solution.py:154
  537.5 5.0 fusion.87
  542.5 5.5 fusion.44
  552.1 7.5 reshape.250
  559.6 5.6 pad.10
  566.2 12.5 %fusion.24 = bf16[960,2560]{1,0:T(8,128)(2,1)} fusion(bf16[768,2560]{1,0:T(8,128)(2,1)} %copy-done.85, bf16[512,2560]{1,0:T(8,128)(2,1)} %copy-done.87, bf16[256,2560]{1,0:T(8,128)(2,1)} %copy-done.82, bf16[768,960]{0,1:T(8,128)(2,1)} %copy-done.42, bf16[512,960]{0,1:T(8,128)(2,1)} %copy-done.26, bf16[256,960]{0,1:T(8,128)(2,1)S(1)} %copy-done.33), kind=kOutput, calls=%fused_computation.29 | convolution fusion | flops 7584645120 | bytes 15728640 | tf_op jit(solution)/shard_map/kd,ke->de/dot_general | solution.py:27
  578.8 7.5 reshape.254
  586.2 5.6 pad.12
  591.9 12.3 %fusion.27 = bf16[960,2560]{1,0:T(8,128)(2,1)} fusion(bf16[768,2560]{1,0:T(8,128)(2,1)} %copy-done.88, bf16[512,2560]{1,0:T(8,128)(2,1)} %get-tuple-element.136, bf16[256,2560]{1,0:T(8,128)(2,1)} %copy-done.83, bf16[768,960]{0,1:T(8,128)(2,1)} %copy-done.42, bf16[512,960]{0,1:T(8,128)(2,1)} %copy-done.26, bf16[256,960]{0,1:T(8,128)(2,1)S(1)} %copy-done.33), kind=kOutput, calls=%fused_computation.30 | convolution fusion | flops 7584645120 | bytes 15728640 | tf_op jit(solution)/shard_map/kd,ke->de/dot_general | solution.py:27
  604.2 7.5 reshape.252
  611.7 5.5 pad.11
  617.9 8.3 multiply_reduce_fusion.2
  627.9 126.1 %reduce-scatter.8.cloned.1.call-done = bf16[32,2560]{1,0:T(8,128)(2,1)} async-done(((bf16[1024,2560]{1,0:T(8,128)(2,1)}), bf16[32,2560]{1,0:T(8,128)(2,1)}) %reduce-scatter.8.cloned.1.call-update) | async-done | bytes 163856 | tf_op jit(solution)/shard_map/reduce_scatter | solution.py:252
  755.7 140.7 %reduce-scatter.12.cloned.1.call-done = bf16[32,2560]{1,0:T(8,128)(2,1)} async-done(((bf16[1024,2560]{1,0:T(8,128)(2,1)}), bf16[32,2560]{1,0:T(8,128)(2,1)}) %reduce-scatter.12.cloned.1.call-update) | async-done | bytes 163856 | tf_op jit(solution)/shard_map/reduce_scatter | solution.py:252
  905.4 133.8 %reduce-scatter.10.cloned.1.call-done = bf16[32,2560]{1,0:T(8,128)(2,1)} async-done(((bf16[1024,2560]{1,0:T(8,128)(2,1)}), bf16[32,2560]{1,0:T(8,128)(2,1)}) %reduce-scatter.10.cloned.1.call-update) | async-done | bytes 163856 | tf_op jit(solution)/shard_map/reduce_scatter | solution.py:252
  1040.8 5.6 add_convert_fusion
  1053.5 5.9 reduce-scatter.16.cloned.1.call-done
  1060.4 12.6 %psum.7 = f32[240,5]{0,1:T(8,128)S(1)} all-reduce(f32[240,5]{0,1:T(8,128)S(1)} %copy.101), channel_id=1, replica_groups=mesh['dp'=8,'fsdp'=4] {'dp'}, use_global_device_ids=true, to_apply=%region_38.39 | all-reduce | flops 1200 | bytes 9600 | tf_op jit(solution)/shard_map/psum | solution.py:339
  1074.1 9.9 all-gather.18.cloned.1.call-done
  1086.8 24.2 %all-gather.26.cloned.1.call-done = bf16[8,30,2560]{2,1,0:T(8,128)(2,1)} async-done(((bf16[1,30,2560]{2,1,0:T(8,128)(2,1)}), bf16[8,30,2560]{2,1,0:T(8,128)(2,1)}) %all-gather.26.cloned.1.call-update) | async-done | bytes 1228816 | tf_op jit(solution)/shard_map/all_gather | solution.py:253
  1116.7 20.6 %all-gather.30.cloned.1.call-done = bf16[8,30,2560]{2,1,0:T(8,128)(2,1)} async-done(((bf16[1,30,2560]{2,1,0:T(8,128)(2,1)}), bf16[8,30,2560]{2,1,0:T(8,128)(2,1)}) %all-gather.30.cloned.1.call-update) | async-done | bytes 1228816 | tf_op jit(solution)/shard_map/all_gather | solution.py:253
  1143.2 20.4 %all-gather.28.cloned.1.call-done = bf16[8,30,2560]{2,1,0:T(8,128)(2,1)} async-done(((bf16[1,30,2560]{2,1,0:T(8,128)(2,1)}), bf16[8,30,2560]{2,1,0:T(8,128)(2,1)}) %all-gather.28.cloned.1.call-update) | async-done | bytes 1228816 | tf_op jit(solution)/shard_map/all_gather | solution.py:253
  (388 shorter events, 157.0 us)
Async XLA Ops:
  7.2 38.8 %copy-start = (bf16[1024,960]{0,1:T(8,128)(2,1)S(1)}, bf16[1024,960]{0,1:T(8,128)(2,1)}, u32[]{:S(2)}) copy-start(bf16[1024,960]{0,1:T(8,128)(2,1)} %param.17) | copy-start | bytes 5898244
  7.2 11.8 %copy-start.72 = (s32[256]{0:T(256)S(1)}, s32[256]{0:T(256)}, u32[]{:S(2)}) copy-start(s32[256]{0:T(256)} %param.31) | copy-start | bytes 3076
  7.2 12.0 %copy-start.76 = (s32[512]{0:T(512)S(1)}, s32[512]{0:T(512)}, u32[]{:S(2)}) copy-start(s32[512]{0:T(512)} %param.30) | copy-start | bytes 6148
  7.2 12.4 %copy-start.74 = (s32[768]{0:T(1024)S(1)}, s32[768]{0:T(1024)}, u32[]{:S(2)}) copy-start(s32[768]{0:T(1024)} %param.29) | copy-start | bytes 9220
  7.2 74.3 %all-gather.20.cloned.1.call-start = ((), (), s32[]{:S(2)}) async-start(), calls=%async_computation.11 | async-start | bytes 5406720 | tf_op jit(solution)/shard_map/all_gather | solution.py:242
  10.2 10.2 copy-start.75
  13.4 135.4 %all-gather.22.cloned.1.call-start = ((), (), s32[]{:S(2)}) async-start(), calls=%async_computation.12 | async-start | bytes 5406720 | tf_op jit(solution)/shard_map/all_gather | solution.py:242
  15.1 10.3 copy-start.77
  15.1 10.3 copy-start.78
  15.1 10.3 copy-start.71
  15.2 201.0 %all-gather.24.cloned.1.call-start = ((), (), s32[]{:S(2)}) async-start(), calls=%async_computation.13 | async-start | bytes 5406720 | tf_op jit(solution)/shard_map/all_gather | solution.py:242
  16.9 266.3 %all-gather.16.cloned.1.call-start = ((), (), s32[]{:S(2)}) async-start(), calls=%async_computation.5 | async-start | bytes 5406720 | tf_op jit(solution)/shard_map/all_gather | solution.py:242
  18.9 608.4 %reduce-scatter.14.cloned.1.call-start = ((), (), s32[]{:S(2)}) async-start(), calls=%async_computation.9 | async-start | bytes 5406720 | tf_op jit(solution)/shard_map/reduce_scatter | solution.py:252
  20.4 29.5 %copy-start.79 = (s32[1024]{0:T(1024)}, s32[1024]{0:T(1024)S(1)}, u32[]{:S(2)}) copy-start(s32[1024]{0:T(1024)S(1)} %fusion.113) | copy-start | bytes 12292
  51.2 38.0 %copy-start.23 = (bf16[768,960]{0,1:T(8,128)(2,1)}, bf16[768,960]{0,1:T(8,128)(2,1)S(1)}, u32[]{:S(2)}) copy-start(bf16[768,960]{0,1:T(8,128)(2,1)S(1)} %multiply_convert_fusion.7) | copy-start | bytes 4423684
  156.5 67.1 %copy-start.38 = (bf16[768,960]{1,0:T(8,128)(2,1)S(1)}, bf16[768,960]{1,0:T(8,128)(2,1)}, u32[]{:S(2)}) copy-start(bf16[768,960]{1,0:T(8,128)(2,1)} %get-tuple-element.27) | copy-start | bytes 4423684
  283.2 12.2 %slice-start.8 = ((s8[4915200]{0:T(1024)(128)(4,1)}), s8[4194304]{0:T(1024)(128)(4,1)S(1)}, s32[]{:S(2)}) async-start(s8[4915200]{0:T(1024)(128)(4,1)} %bitcast.94), calls=%async_computation.26 | async-start | bytes 8388608
  283.2 12.2 %slice-start.9 = ((s8[4915200]{0:T(1024)(128)(4,1)}), s8[720896]{0:T(1024)(128)(4,1)S(1)}, s32[]{:S(2)}) async-start(s8[4915200]{0:T(1024)(128)(4,1)} %bitcast.94), calls=%async_computation.27 | async-start | bytes 1441792
  328.8 13.2 %slice-start.16 = ((s8[5242880]{0:T(1024)(128)(4,1)}), s8[4194304]{0:T(1024)(128)(4,1)S(1)}, s32[]{:S(2)}) async-start(s8[5242880]{0:T(1024)(128)(4,1)} %bitcast.105), calls=%async_computation.34 | async-start | bytes 8388608
  328.8 19.4 %slice-start.10 = ((s8[4915200]{0:T(1024)(128)(4,1)}), s8[4194304]{0:T(1024)(128)(4,1)S(1)}, s32[]{:S(2)}) async-start(s8[4915200]{0:T(1024)(128)(4,1)} %bitcast.96), calls=%async_computation.28 | async-start | bytes 8388608
  331.8 16.4 %slice-start.11 = ((s8[4915200]{0:T(1024)(128)(4,1)}), s8[720896]{0:T(1024)(128)(4,1)S(1)}, s32[]{:S(2)}) async-start(s8[4915200]{0:T(1024)(128)(4,1)} %bitcast.96), calls=%async_computation.29 | async-start | bytes 1441792
  365.6 16.3 %copy-start.14 = (f32[256,960]{0,1:T(8,128)}, f32[256,960]{0,1:T(8,128)S(1)}, u32[]{:S(2)}) copy-start(f32[256,960]{0,1:T(8,128)S(1)} %get-tuple-element.128) | copy-start | bytes 2949124
  400.8 20.4 %copy-start.10 = (f32[256,960]{0,1:T(8,128)}, f32[256,960]{0,1:T(8,128)S(1)}, u32[]{:S(2)}) copy-start(f32[256,960]{0,1:T(8,128)S(1)} %get-tuple-element.141) | copy-start | bytes 2949124
  400.8 11.2 slice-start.4
  400.8 16.6 %slice-start.24 = ((s8[4915200]{0:T(1024)(128)(4,1)}), s8[4194304]{0:T(1024)(128)(4,1)S(1)}, s32[]{:S(2)}) async-start(s8[4915200]{0:T(1024)(128)(4,1)} %bitcast.113), calls=%async_computation.42 | async-start | bytes 8388608
  401.4 10.6 copy-start.47
  401.4 10.6 slice-start.5
  401.4 16.1 %slice-start.25 = ((s8[4915200]{0:T(1024)(128)(4,1)}), s8[720896]{0:T(1024)(128)(4,1)S(1)}, s32[]{:S(2)}) async-start(s8[4915200]{0:T(1024)(128)(4,1)} %bitcast.113), calls=%async_computation.43 | async-start | bytes 1441792
  412.0 11.4 slice-start.12
  427.8 20.3 %copy-start.9 = (f32[768,960]{0,1:T(8,128)S(1)}, f32[768,960]{0,1:T(8,128)}, u32[]{:S(2)}) copy-start(f32[768,960]{0,1:T(8,128)} %copy-done.7) | copy-start | bytes 8847364
  458.6 21.5 %slice-start.6 = ((s8[4915200]{0:T(1024)(128)(4,1)}), s8[720896]{0:T(1024)(128)(4,1)S(1)}, s32[]{:S(2)}) async-start(s8[4915200]{0:T(1024)(128)(4,1)} %bitcast.92), calls=%async_computation.24 | async-start | bytes 1441792
  469.0 285.0 %reduce-scatter.8.cloned.1.call-start = ((), (), s32[]{:S(2)}) async-start(), calls=%async_computation.6 | async-start | bytes 5406720 | tf_op jit(solution)/shard_map/reduce_scatter | solution.py:252
  469.1 11.0 slice-start.7
  480.2 15.1 %slice-start.14 = ((s8[4915200]{0:T(1024)(128)(4,1)}), s8[4194304]{0:T(1024)(128)(4,1)S(1)}, s32[]{:S(2)}) async-start(s8[4915200]{0:T(1024)(128)(4,1)} %bitcast.100), calls=%async_computation.32 | async-start | bytes 8388608
  484.3 11.0 slice-start.15
  500.7 36.7 %copy-start.39 = (bf16[768,960]{1,0:T(8,128)(2,1)S(1)}, bf16[768,960]{1,0:T(8,128)(2,1)}, u32[]{:S(2)}) copy-start(bf16[768,960]{1,0:T(8,128)(2,1)} %get-tuple-element.27) | copy-start | bytes 4423684
  500.7 36.7 %copy-start.41 = (bf16[768,960]{0,1:T(8,128)(2,1)S(1)}, bf16[768,960]{0,1:T(8,128)(2,1)}, u32[]{:S(2)}) copy-start(bf16[768,960]{0,1:T(8,128)(2,1)} %copy-done.40) | copy-start | bytes 4423684
  500.7 36.7 %copy-start.45 = (bf16[512,960]{1,0:T(8,128)(2,1)S(1)}, bf16[512,960]{1,0:T(8,128)(2,1)}, u32[]{:S(2)}) copy-start(bf16[512,960]{1,0:T(8,128)(2,1)} %get-tuple-element.28) | copy-start | bytes 2949124
  500.7 36.7 %copy-start.50 = (bf16[256,960]{1,0:T(8,128)(2,1)S(1)}, bf16[256,960]{1,0:T(8,128)(2,1)}, u32[]{:S(2)}) copy-start(bf16[256,960]{1,0:T(8,128)(2,1)} %get-tuple-element.29) | copy-start | bytes 1474564
  565.2 331.1 %reduce-scatter.12.cloned.1.call-start = ((), (), s32[]{:S(2)}) async-start(), calls=%async_computation.8 | async-start | bytes 5406720 | tf_op jit(solution)/shard_map/reduce_scatter | solution.py:252
  591.8 447.3 %reduce-scatter.10.cloned.1.call-start = ((), (), s32[]{:S(2)}) async-start(), calls=%async_computation.7 | async-start | bytes 5406720 | tf_op jit(solution)/shard_map/reduce_scatter | solution.py:252
  617.2 442.2 %reduce-scatter.16.cloned.1.call-start = ((), (), s32[]{:S(2)}) async-start(), calls=%async_computation.17 | async-start | bytes 614400
  627.2 413.5 %copy-start.64 = (f32[960,1]{0,1:T(1,128)S(1)}, f32[960,1]{0,1:T(1,128)}, u32[]{:S(2)}) copy-start(f32[960,1]{0,1:T(1,128)} %copy-done.63) | copy-start | bytes 11524
  627.3 456.8 %all-gather.18.cloned.1.call-start = ((), (), s32[]{:S(2)}) async-start(), calls=%async_computation.10 | async-start | bytes 1474560 | tf_op jit(solution)/shard_map/all_gather | solution.py:253
  627.9 483.1 %all-gather.26.cloned.1.call-start = ((), (), s32[]{:S(2)}) async-start(), calls=%async_computation.14 | async-start | bytes 1474560 | tf_op jit(solution)/shard_map/all_gather | solution.py:253
  755.6 381.6 %all-gather.30.cloned.1.call-start = ((), (), s32[]{:S(2)}) async-start(), calls=%async_computation.16 | async-start | bytes 1474560 | tf_op jit(solution)/shard_map/all_gather | solution.py:253
  898.0 265.6 %all-gather.28.cloned.1.call-start = ((), (), s32[]{:S(2)}) async-start(), calls=%async_computation.15 | async-start | bytes 1474560 | tf_op jit(solution)/shard_map/all_gather | solution.py:253
  1137.2 29.0 %copy-start.1 = (bf16[1024,960]{0,1:T(8,128)(2,1)S(1)}, bf16[1024,960]{0,1:T(8,128)(2,1)}, u32[]{:S(2)}) copy-start(bf16[1024,960]{0,1:T(8,128)(2,1)} %param.17) | copy-start | bytes 5898244
  (80 other events, 336.1 us)
Sparse Core Ops, SparseCore 0:
  13.5 68.0 all-gather.19
  85.0 63.7 all-gather.21
  152.3 63.7 all-gather.23
  219.4 63.7 all-gather.15
  469.2 142.6 reduce-scatter.13
  614.0 139.9 reduce-scatter.7
  756.3 139.9 reduce-scatter.11
  898.6 140.4 reduce-scatter.9
  1042.0 17.3 reduce-scatter.15
  1061.1 22.8 all-gather.17
  1086.5 24.4 all-gather.25
  1112.7 24.4 all-gather.29
  1139.1 24.4 all-gather.27

commit v2 on v1

--- a/solution.py
+++ b/solution.py
@@ -234,6 +234,447 @@
     return grad_rows, pairs, (gain_attn_grad, gain_ffn_grad, router_grad)
 
 
+MESH = pl.DeviceIdType.MESH
+GATHER_ORDER = (0, 1, 2, 3)
+
+
+def place():
+    d, z = lax.axis_index("dp"), lax.axis_index("fsdp")
+    c, x, y = lax.rem(d, 2), lax.rem(lax.div(d, 2), 2), lax.div(d, 4)
+    ids = dict(
+        core={"dp": d + 1 - 2 * c},
+        x={"dp": d + 2 - 4 * x},
+        y={"dp": d + 4 - 8 * y},
+        up={"fsdp": z + 1},
+        down={"fsdp": z - 1},
+    )
+    return z, c, x, y, ids
+
+
+def greet(z, ids):
+    barrier = pltpu.get_barrier_semaphore()
+    for name in ("core", "x", "y"):
+        pl.semaphore_signal(barrier, inc=1, device_id=ids[name], device_id_type=MESH)
+
+    @pl.when(z < 3)
+    def _():
+        pl.semaphore_signal(barrier, inc=1, device_id=ids["up"], device_id_type=MESH)
+
+    @pl.when(z > 0)
+    def _():
+        pl.semaphore_signal(barrier, inc=1, device_id=ids["down"], device_id_type=MESH)
+
+    pl.semaphore_wait(barrier, 5 - lax.div(z, 3) - lax.div(3 - z, 3))
+
+
+def remote(src, dst, send, recv, target):
+    return pltpu.make_async_remote_copy(
+        src_ref=src, dst_ref=dst, send_sem=send, recv_sem=recv, device_id=target, device_id_type=MESH
+    )
+
+
+def piece(ref, a, lead, p, parts=4):
+    if a < 3:
+        width = ref.shape[-1] // parts
+        return ref.at[(*lead, slice(None), pl.ds(pl.multiple_of(p * width, 128), width))]
+    height = ref.shape[-2] // parts
+    return ref.at[(*lead, pl.ds(pl.multiple_of(p * height, 16), height), slice(None))]
+
+
+def pieces_of(a, x, y):
+    f, s, wf, ws = (y, x, 2, 1) if a < 2 else (x, y, 2, 1)
+    own = 2 * f + s
+    nx = 2 * f + 1 - s if a < 2 else 2 * (1 - f) + s
+    ny = 2 * (1 - f) + s if a < 2 else 2 * f + 1 - s
+    return own, nx, ny, 2 * (1 - f) + 1 - s
+
+
+def plane_stage(stage, refs, a, slot, lead, where, send, recv):
+    z, c, x, y, ids = where
+    own, nx, ny, far = pieces_of(a, x, y)
+    first = [(own, "x", 0), (own, "y", 1), (own, "core", 3)]
+    second = [(nx, "core", 4), (ny, "core", 5), (ny, "x", 2) if a < 2 else (nx, "y", 2)]
+    third = [(far, "core", 6)]
+
+    def copy(p, name, kind):
+        part = piece(refs[a], a, lead, p)
+        return remote(part, part, send.at[kind, a, slot], recv.at[kind, a, slot], ids[name])
+
+    def arrived(p, kind):
+        part = piece(refs[a], a, lead, p)
+        remote(part, part, send.at[kind, a, slot], recv.at[kind, a, slot], ids["core"]).wait_recv()
+
+    if stage == 1:
+        for item in first:
+            copy(*item).start()
+    elif stage == 2:
+        arrived(nx, 0)
+        copy(*second[0]).start()
+        arrived(ny, 1)
+        copy(*second[1]).start()
+        copy(*second[2]).start()
+    elif stage == 3:
+        arrived(far, 2)
+        copy(*third[0]).start()
+    else:
+        other = (*lead[:-1], 1 - c)
+        for p, kind in ((own, 3), (nx, 4), (ny, 5), (far, 6)):
+            part = piece(refs[a], a, other, p)
+            remote(part, part, send.at[kind, a, slot], recv.at[kind, a, slot], ids["core"]).wait_recv()
+        for item in first + second + third:
+            copy(*item).wait_send()
+
+
+def gather_kernel(s0, s1, s2, s3, small, o0, o1, o2, o3, small_out, send, recv, zsend, zrecv, local):
+    where = place()
+    z, c, x, y, ids = where
+    shards, outs = (s0, s1, s2, s3), (o0, o1, o2, o3)
+    greet(z, ids)
+
+    def along(a, origin, way):
+        if a == 4:
+            dst = small_out.at[origin]
+            src = dst
+        else:
+            dst = src = piece(outs[a], a, (origin, c), pieces_of(a, x, y)[0])
+        way_index = 0 if way == "up" else 1
+        return src, dst, zsend.at[way_index, a, origin], zrecv.at[a, origin], ids[way]
+
+    def own_copy(a, way):
+        src, dst, ss, rs, target = along(a, z, way)
+        src = small if a == 4 else piece(shards[a], a, (c,), pieces_of(a, x, y)[0])
+        return remote(src, dst, ss, rs, target)
+
+    kinds = (4,) + GATHER_ORDER
+
+    @pl.when(z < 3)
+    def _():
+        for a in kinds:
+            own_copy(a, "up").start()
+
+    @pl.when(z > 0)
+    def _():
+        for a in kinds:
+            own_copy(a, "down").start()
+
+    def own_local(a):
+        if a == 4:
+            return pltpu.make_async_copy(small, small_out.at[z], local.at[a])
+        return pltpu.make_async_copy(shards[a], outs[a].at[z], local.at[a])
+
+    for a in kinds:
+        own_local(a).start()
+
+    def foreign(step, a, stage):
+        for way, origin, there, more in (
+            ("up", z - step, z >= step, z < 3),
+            ("down", z + step, z <= 3 - step, z > 0),
+        ):
+
+            @pl.when(there)
+            def _():
+                if stage == 1:
+                    remote(*along(a, origin, way)).wait_recv()
+
+                    @pl.when(more)
+                    def _():
+                        remote(*along(a, origin, way)).start()
+
+                if a < 4:
+                    plane_stage(stage, outs, a, origin, (origin, c), where, send, recv)
+                if stage == 4:
+
+                    @pl.when(more)
+                    def _():
+                        remote(*along(a, origin, way)).wait_send()
+
+    for step in (1, 2, 3):
+        foreign(step, 4, 1)
+    events = [(step, a) for step in (1, 2, 3) for a in GATHER_ORDER]
+    for k in range(len(events) + 4):
+        if k < len(events):
+            foreign(*events[k], 1)
+        if 2 <= k < len(events) + 2:
+            foreign(*events[k - 2], 2)
+        if 4 <= k:
+            foreign(*events[k - 4], 3)
+    for a in kinds:
+        for step in (1, 2, 3):
+            foreign(step, a, 4)
+
+    @pl.when(z < 3)
+    def _():
+        for a in kinds:
+            own_copy(a, "up").wait_send()
+
+    @pl.when(z > 0)
+    def _():
+        for a in kinds:
+            own_copy(a, "down").wait_send()
+
+    for a in kinds:
+        own_local(a).wait()
+
+
+def gather_weights(shards, small):
+    dma = pltpu.SemaphoreType.DMA
+    vmem, hbm = pl.BlockSpec(memory_space=pltpu.VMEM), pl.BlockSpec(memory_space=pl.ANY)
+    halves = [s.reshape(2, s.shape[0] // 2, s.shape[1]) for s in shards]
+    out = pl.pallas_call(
+        gather_kernel,
+        out_shape=tuple(jax.ShapeDtypeStruct((4, *s.shape), s.dtype) for s in halves + [small]),
+        in_specs=[vmem] * 5,
+        out_specs=[hbm] * 5,
+        scratch_shapes=[dma((7, 4, 4)), dma((7, 4, 4)), dma((2, 5, 4)), dma((5, 4)), dma((5,))],
+        compiler_params=pltpu.CompilerParams(collective_id=0, has_side_effects=True, vmem_limit_bytes=32 << 20),
+        name="gather_weights",
+    )(*halves, small)
+    return [o.reshape(-1, o.shape[-1]) for o in out[:4]], out[4]
+
+
+TARGETS = (3, 0, 2, 1)
+
+
+def add_into(dst, dlead, drow, dcol, src, slead, rows, cols):
+    wide = cols % 640 == 0
+    count = cols // 640 if wide else rows // 80
+
+    def one(i):
+        if wide:
+            shift = pl.multiple_of(i * 640, 128)
+            at_src = (*slead, slice(None), pl.ds(shift, 640))
+            at_dst = (*dlead, slice(None), pl.ds(pl.multiple_of(dcol + shift, 128), 640))
+        else:
+            shift = pl.multiple_of(i * 80, 16)
+            at_src = (*slead, pl.ds(shift, 80), slice(None))
+            at_dst = (*dlead, pl.ds(pl.multiple_of(drow + shift, 16), 80), slice(None))
+        dst[at_dst] = (dst[at_dst].astype(f32) + src[at_src].astype(f32)).astype(dst.dtype)
+
+    if count == 1:
+        one(0)
+    else:
+
+        @pl.loop(0, count)
+        def _(i):
+            one(i)
+
+
+def reduce_kernel(
+    g0, g1, g2, g3, small, o0, o1, o2, o3, small_out,
+    a0, a1, a2, a3, c0, c1, c2, c3, p0, p1, p2, p3, q0, q1, q2, q3, u0, u1, u2, u3, d0, d1, d2, d3,
+    small_in, small_out_buf, csend, crecv, psend, precv, zsend, zrecv, send, recv, loads, ssend, srecv,
+):
+    where = place()
+    z, c, x, y, ids = where
+    full, outs, acc, cbuf = (g0, g1, g2, g3), (o0, o1, o2, o3), (a0, a1, a2, a3), (c0, c1, c2, c3)
+    first, second = (p0, p1, p2, p3), (q0, q1, q2, q3)
+    up, down = (u0, u1, u2, u3), (d0, d1, d2, d3)
+    greet(z, ids)
+
+    def load(a, t):
+        return pltpu.make_async_copy(full[a].at[t, c], acc[a].at[t], loads.at[a, t])
+
+    def core_copy(a, t):
+        return remote(full[a].at[t, 1 - c], cbuf[a].at[t], csend.at[a, t], crecv.at[a, t], ids["core"])
+
+    def coords(a):
+        return (y, x, "y", "x") if a < 2 else (x, y, "x", "y")
+
+    def first_copy(a, t):
+        f, s, nf, ns = coords(a)
+        return remote(piece(acc[a], a, (t,), 1 - f, 2), first[a].at[t], psend.at[0, a, t], precv.at[0, a, t], ids[nf])
+
+    def second_copy(a, t):
+        f, s, nf, ns = coords(a)
+        return remote(
+            piece(acc[a], a, (t,), 2 * f + 1 - s), second[a].at[t], psend.at[1, a, t], precv.at[1, a, t], ids[ns]
+        )
+
+    def own_piece(a, t):
+        f, s, nf, ns = coords(a)
+        return piece(acc[a], a, (t,), 2 * f + s)
+
+    def up_copy(a, t):
+        return remote(own_piece(a, t), up[a].at[t], zsend.at[0, a, t], zrecv.at[0, a, t], ids["up"])
+
+    def down_copy(a, t):
+        return remote(own_piece(a, t), down[a].at[t], zsend.at[1, a, t], zrecv.at[1, a, t], ids["down"])
+
+    def add_piece(a, t, src, index, parts):
+        rows, cols = src.shape[-2:]
+        offset = index * (acc[a].shape[-1] // parts if a < 3 else acc[a].shape[-2] // parts)
+        add_into(acc[a], (t,), 0 if a < 3 else offset, offset if a < 3 else 0, src, (t,), rows, cols)
+
+    def stage2(t):
+        for a in range(4):
+            load(a, t).wait()
+            core_copy(a, t).wait_recv()
+            add_piece(a, t, cbuf[a], 0, 1)
+            first_copy(a, t).start()
+
+    def stage3(t):
+        for a in range(4):
+            first_copy(a, t).wait_recv()
+            add_piece(a, t, first[a], coords(a)[0], 2)
+            second_copy(a, t).start()
+
+    def own_index(a):
+        f, s, nf, ns = coords(a)
+        return 2 * f + s
+
+    def stage4(t):
+        for a in range(4):
+            second_copy(a, t).wait_recv()
+            add_piece(a, t, second[a], own_index(a), 4)
+
+            if t > 0:
+
+                @pl.when(z == 0)
+                def _():
+                    up_copy(a, t).start()
+
+            if t < 3:
+
+                @pl.when(z == 3)
+                def _():
+                    down_copy(a, t).start()
+
+    def stage5(t):
+        for a in range(4):
+            if t > 0:
+
+                @pl.when((z > 0) & (z <= t))
+                def _():
+                    up_copy(a, t).wait_recv()
+                    add_piece(a, t, up[a], own_index(a), 4)
+
+                @pl.when((z > 0) & (z < t))
+                def _():
+                    up_copy(a, t).start()
+
+            if t < 3:
+
+                @pl.when((z < 3) & (z >= t))
+                def _():
+                    down_copy(a, t).wait_recv()
+                    add_piece(a, t, down[a], own_index(a), 4)
+
+                @pl.when((z < 3) & (z > t))
+                def _():
+                    down_copy(a, t).start()
+
+    def small_copy(k, name):
+        return remote(small_out_buf.at[k], small_in.at[k], ssend.at[k], srecv.at[k], ids[name])
+
+    for t in TARGETS:
+        for a in range(4):
+            core_copy(a, t).start()
+            load(a, t).start()
+    total = small[...]
+    for k, name in enumerate(("core", "x", "y")):
+        small_out_buf[k] = total
+        small_copy(k, name).start()
+        small_copy(k, name).wait_recv()
+        total = total + small_in[k]
+    small_out[...] = total
+
+    n = len(TARGETS)
+    for k in range(n + 3):
+        if k < n:
+            stage2(TARGETS[k])
+        if 1 <= k < n + 1:
+            stage3(TARGETS[k - 1])
+        if 2 <= k < n + 2:
+            stage4(TARGETS[k - 2])
+        if 3 <= k:
+            stage5(TARGETS[k - 3])
+
+    small_out_buf[3] = small_out[...]
+    small_out_buf[4] = small_out[...]
+
+    @pl.when(z > 0)
+    def _():
+        small_copy(3, "up").wait_recv()
+        small_out_buf[3] = small_out_buf[3] + small_in[3]
+
+    @pl.when(z < 3)
+    def _():
+        small_copy(3, "up").start()
+        small_copy(4, "down").wait_recv()
+        small_out_buf[4] = small_out_buf[4] + small_in[4]
+
+    @pl.when(z > 0)
+    def _():
+        small_copy(4, "down").start()
+
+    small_out[...] = small_out_buf[3] + small_out_buf[4] - small_out[...]
+
+    for a in range(4):
+        src = own_piece(a, z)
+        dst = piece(outs[a], a, (c,), own_index(a))
+        dst[...] = src[...]
+        plane_stage(1, outs, a, 0, (c,), where, send, recv)
+    for stage in (2, 3, 4):
+        for a in range(4):
+            plane_stage(stage, outs, a, 0, (c,), where, send, recv)
+
+    for k, name in enumerate(("core", "x", "y")):
+        small_copy(k, name).wait_send()
+
+    @pl.when(z < 3)
+    def _():
+        small_copy(3, "up").wait_send()
+
+    @pl.when(z > 0)
+    def _():
+        small_copy(4, "down").wait_send()
+
+    for t in range(4):
+        for a in range(4):
+            core_copy(a, t).wait_send()
+            first_copy(a, t).wait_send()
+            second_copy(a, t).wait_send()
+            if t > 0:
+
+                @pl.when(z < t)
+                def _():
+                    up_copy(a, t).wait_send()
+
+            if t < 3:
+
+                @pl.when(z > t)
+                def _():
+                    down_copy(a, t).wait_send()
+
+
+def reduce_grads(grads, small):
+    dma = pltpu.SemaphoreType.DMA
+    vmem, hbm = pl.BlockSpec(memory_space=pltpu.VMEM), pl.BlockSpec(memory_space=pl.ANY)
+    full = [g.reshape(4, 2, g.shape[0] // 8, g.shape[1]) for g in grads]
+
+    def buffers(parts):
+        shapes = []
+        for a, g in enumerate(full):
+            rows, cols = g.shape[2:]
+            shapes.append((4, rows, cols // parts) if a < 3 else (4, rows // parts, cols))
+        return [pltpu.VMEM(s, bf16) for s in shapes]
+
+    out = pl.pallas_call(
+        reduce_kernel,
+        out_shape=tuple(jax.ShapeDtypeStruct(g.shape[1:], bf16) for g in full)
+        + (jax.ShapeDtypeStruct(small.shape, f32),),
+        in_specs=[hbm] * 4 + [vmem],
+        out_specs=[vmem] * 5,
+        scratch_shapes=buffers(1) + buffers(1) + buffers(2) + buffers(4) + buffers(4) + buffers(4)
+        + [pltpu.VMEM((5, *small.shape), f32)] * 2
+        + [dma((4, 4)), dma((4, 4)), dma((2, 4, 4)), dma((2, 4, 4)), dma((2, 4, 4)), dma((2, 4, 4))]
+        + [dma((7, 4, 1)), dma((7, 4, 1)), dma((4, 4)), dma((5,)), dma((5,))],
+        compiler_params=pltpu.CompilerParams(collective_id=1, has_side_effects=True, vmem_limit_bytes=60 << 20),
+        name="reduce_grads",
+    )(*full, small)
+    return [o.reshape(-1, o.shape[-1]) for o in out[:4]], out[4]
+
+
 def gather_all(shard):
     if shard.shape[0] % lax.axis_size("dp"):
         return lax.all_gather(shard, "fsdp", axis=0, tiled=True)
@@ -261,12 +702,19 @@
     counts = tuple(p.shape[0] for p in picks)
     tokens = inputs.shape[0]
 
-    gathered1 = gather_all(jnp.concatenate([w_out, w_query, w_key, w_value], axis=1))
-    wg, wu, wd = gather_all(w_gate), gather_all(w_up), gather_all(w_down)
-    wo, wqkv = gathered1[:, :QW], gathered1[:, QW:]
-    small = jnp.concatenate([gain_attn[:, None], gain_ffn[:, None], w_router], axis=1)
-    small = lax.all_gather(small, "fsdp", axis=0, tiled=True).astype(f32)
-    weights = (wqkv, wo, wg, wu, wd, small[:, 0], small[:, 1], small[:, 2:5])
+    by_kernel = lax.axis_size("dp") == 8 and lax.axis_size("fsdp") == 4
+    owned = gain_attn.shape[0]
+    first = jnp.concatenate([w_out, w_query, w_key, w_value], axis=1)
+    small = jnp.concatenate([gain_attn[None], gain_ffn[None], w_router.T], axis=0)
+    if by_kernel:
+        small = jnp.pad(small, ((0, 16 - small.shape[0]), (0, -owned % 128)))
+        (first, wg, wu, wd), small = gather_weights([first, w_gate, w_up, w_down], small)
+        small = small[:, :, :owned].transpose(1, 0, 2).reshape(16, -1).astype(f32)
+    else:
+        first, wg, wu, wd = gather_all(first), gather_all(w_gate), gather_all(w_up), gather_all(w_down)
+        small = lax.all_gather(small, "fsdp", axis=1, tiled=True).astype(f32)
+    wo, wqkv = first[:, :QW], first[:, QW:]
+    weights = (wqkv, wo, wg, wu, wd, small[0], small[1], small[2 : 2 + NREC].T)
 
     places = jnp.arange(tokens, dtype=jnp.int32)
     level = jnp.full((tokens,), NREC, jnp.int32)
@@ -328,15 +776,20 @@
         right = jnp.concatenate([p[i][1] for p in pairs], axis=0)
         sums.append(dot("kd,ke->de", left, right).astype(bf16))
     down, gate, up, out, qkv = sums
-    down, gate, up = reduce_all(down), reduce_all(gate), reduce_all(up)
-    first = reduce_all(jnp.concatenate([out, qkv], axis=1)).astype(f32)
+    first = jnp.concatenate([out, qkv], axis=1)
     small = jnp.stack(
         [smalls[0][0] + smalls[1][0] + smalls[2][0], smalls[0][1] + smalls[1][1] + smalls[2][1]]
-        + [s[2] for s in reversed(smalls)],
-        axis=1,
+        + [s[2] for s in reversed(smalls)]
     )
-    small = lax.psum_scatter(small, "fsdp", scatter_dimension=0, tiled=True)
-    small = lax.psum(small, "dp")
+    if by_kernel:
+        small = jnp.pad(small, ((0, 8 - small.shape[0]), (0, -small.shape[1] % 128)))
+        (first, gate, up, down), small = reduce_grads([first, gate, up, down], small)
+        small = lax.dynamic_slice_in_dim(small, lax.axis_index("fsdp") * owned, owned, 1)
+    else:
+        first, gate, up, down = reduce_all(first), reduce_all(gate), reduce_all(up), reduce_all(down)
+        small = lax.psum_scatter(small, "fsdp", scatter_dimension=1, tiled=True)
+        small = lax.psum(small, "dp")
+    first = first.astype(f32)
     return (
         result,
         grad_inputs,
@@ -347,9 +800,9 @@
         gate.astype(f32),
         up.astype(f32),
         down.astype(f32),
-        small[:, 0],
-        small[:, 1],
-        small[:, 2:5],
+        small[0],
+        small[1],
+        small[2 : 2 + NREC].T,
     )
 
 

time: 1180 us -> 711 us (0.60)
  waiting for transfers between devices: 621 us -> 0 us
  Pallas kernels: 137 us -> 395 us
  local copies, waits for them, and re-layouts: 132 us -> 53.8 us
  blocking collectives: 27.5 us -> 0 us
  other arithmetic: 26.6 us -> 43.5 us
  between operations: 15.8 us -> 2.68 us
    reduce_scatter x4 -> x0, waiting for transfers between devices: 401 us -> none  [reduce_all(): lax.psum_scatter(padded.reshape(-1, total.shape[1]), ('fsdp', 'dp'), scat...]
    pallas_call x0 -> x2, Pallas kernels: none -> 258 us  [the longest x1 168 us: reduce_grads(): pl.pallas_call(reduce_kernel, out_shape=tuple((jax.ShapeDtypeStruct(g.sha...]
    all_gather x8 -> x0, waiting for transfers between devices: 214 us -> none  [the longest x4 139 us: gather_all(): return lax.all_gather(part, ('fsdp', 'dp'), axis=0, tiled=True)]
    unnamed x247 -> x254, local copies, waits for them, and re-layouts: 58.4 us -> 24.1 us
    reshape x3 -> x0, local copies, waits for them, and re-layouts: 22.4 us -> none  [reduce_all(): total.reshape(chunks, rows, -1)]
    pad x3 -> x1, local copies, waits for them, and re-layouts: 16.6 us -> 0.62 us  [body(): jnp.pad(small, ((0, 8 - small.shape[0]), (0, -small.shape[1] % 128)))]
    all_gather x1 -> x0, blocking collectives: 14.9 us -> none  [body(): small = lax.all_gather(small, 'fsdp', axis=0, tiled=True).astype(f32)]
    psum x1 -> x0, blocking collectives: 12.6 us -> none  [body(): small = lax.psum(small, 'dp')]
  transfers between devices with their start and end apart: 13 -> 0, of which waited for: 12 -> 0; matrix products, arithmetic and copies ran while one was open for 20% -> 0% of each run, Pallas kernels for 6% -> 0%
where the time goes in v2:
time: 711 us; the launch traced here: 705 us
  Pallas kernels  395 us (56%)
  matrix products  210 us (30%)
  local copies, waits for them, and re-layouts  53.8 us (8%)
  other arithmetic  43.5 us (6%)
    dot_general x40, matrix products, dot(): return jnp.einsum(spec, left, right, preferred_element_type=f32)  210 us
    pallas_call x1, Pallas kernels, reduce_grads(): pl.pallas_call(reduce_kernel, out_shape=tuple((jax.ShapeDtypeStruct(g.sha...  168 us
    pallas_call x1, Pallas kernels, gather_weights(): pl.pallas_call(gather_kernel, out_shape=tuple((jax.ShapeDtypeStruct((4, *...  90 us
    pallas_call x3, Pallas kernels, attend_fwd(): pl.pallas_call(attend_fwd_kernel, grid=(k // ROWS,), out_shape=(jax.Shape...  73.2 us
    pallas_call x3, Pallas kernels, attend_bwd(): pl.pallas_call(attend_bwd_kernel, grid=(count // ROWS,), out_shape=jax.Sh...  64.4 us
    unnamed x254, local copies, waits for them, and re-layouts  24.1 us

profile of v2, /device:TPU:0, one launch (start us, length us, event | category | flops | bytes accessed | tf_op | source)
XLA Modules:
  0.0 705.5 jit_solution(7506092151651472172)
XLA Ops:
  4.3 4.2 fusion.42
  14.0 90.0 %gather_weights.1 = (bf16[4,2,120,2560]{3,2,1,0:T(8,128)(2,1)S(1)}, bf16[4,2,120,2560]{3,2,1,0:T(8,128)(2,1)S(1)}, bf16[4,2,120,2560]{3,2,1,0:T(8,128)(2,1)S(1)}...) custom-call(bf16[2,120,2560]{2,1,0:T(8,128)(2,1)S(1)} %bitcast.127, bf16[2,120,2560]{2,1,0:T(8,128)(2,1)S(1)} %bitcast.128, ...), custom_call_target="tpu_custom_call" | custom-call | tf_op jit(solution)/shard_map/gather_weights/pallas_call | solution.py:423
  115.8 7.7 %fusion.108.qkv_ref = f32[768,1600]{1,0:T(8,128)} fusion(bf16[768,960]{0,1:T(8,128)(2,1)S(1)} %multiply_convert_fusion.7, bf16[960,2560]{1,0:T(8,128)(2,1)} %bitcast.106), kind=kOutput, calls=%fused_computation.157 | convolution fusion | flops 2359296000 | bytes 9584640 | tf_op jit(solution)/shard_map/kd,de->ke/dot_general | solution.py:27
  129.6 36.0 %attend_fwd.3 = (bf16[768,960]{1,0:T(8,128)(2,1)}, bf16[15,768,64]{2,1,0:T(8,128)(2,1)}, bf16[5,768,64]{2,1,0:T(8,128)(2,1)}, bf16[5,768,64]{2,1,0:T(8,128)(2,1)}, f32[16,768]{1,0:T(8,128)}) custom-call(f32[768,1600]{1,0:T(8,128)} %fusion.108.qkv_ref, f32[768,64]{1,0:T(8,128)} %get-tuple-element.205.cos_ref, f32[768,64]{1,0:T(8,128)} %get-tuple-element.204.sin_ref, ...), custom_call_target="tpu_custom_call" | custom-call | tf_op jit(solution)/shard_map/attend_fwd/pallas_call | solution.py:78
  165.7 6.3 multiply_reduce_fusion.6
  174.4 7.0 fusion.150
  181.5 7.8 %multiply_convert_fusion.2 = (bf16[768,2560]{1,0:T(8,128)(2,1)}, bf16[768,2560]{1,0:T(8,128)(2,1)}) fusion(f32[768,2560]{1,0:T(8,128)S(1)} %fusion.150, bf16[768,960]{0,1:T(8,128)(2,1)S(1)} %multiply_convert_fusion.6, bf16[960,2560]{1,0:T(8,128)(2,1)S(1)} %bitcast.132), kind=kOutput, calls=%fused_computation.25 | convolution fusion | flops 3788636160 | bytes 22118400 | tf_op jit(solution)/shard_map/kd,df->kf/dot_general | solution.py:27
  189.3 10.9 %multiply_add_fusion = (f32[768,960]{0,1:T(8,128)S(1)}, f32[768,960]{0,1:T(8,128)}) fusion(f32[1024,960]{0,1:T(8,128)S(1)} %copy-done.9, f32[768]{0:T(1024)S(1)} %get-tuple-element.203, f32[768,960]{0,1:T(8,128)} %get-tuple-element.181, bf16[768,2560]{1,0:T(8,128)(2,1)} %get-tuple-element.182, bf16[2560,960]{1,0:T(8,128)(2,1)} %bitcast.148), kind=kOutput, calls=%fused_computation.90 | convolution fusion | flops 3777085440 | bytes 20646912 | tf_op jit(solution)/shard_map/kf,fd->kd/dot_general | solution.py:27
  200.8 4.0 fusion.106.qkv_ref
  207.1 25.4 %attend_fwd.4 = (bf16[512,960]{1,0:T(8,128)(2,1)}, bf16[15,512,64]{2,1,0:T(8,128)(2,1)}, bf16[5,512,64]{2,1,0:T(8,128)(2,1)}, bf16[5,512,64]{2,1,0:T(8,128)(2,1)}, f32[16,512]{1,0:T(8,128)}) custom-call(f32[512,1600]{1,0:T(8,128)} %fusion.106.qkv_ref, f32[512,64]{1,0:T(8,128)} %get-tuple-element.207.cos_ref, f32[512,64]{1,0:T(8,128)} %get-tuple-element.206.sin_ref, ...), custom_call_target="tpu_custom_call" | custom-call | tf_op jit(solution)/shard_map/attend_fwd/pallas_call | solution.py:78
  232.6 3.9 multiply_reduce_fusion.15
  236.8 4.7 fusion.151
  241.6 7.3 %multiply_convert_fusion.5 = (bf16[512,2560]{1,0:T(8,128)(2,1)}, bf16[512,2560]{1,0:T(8,128)(2,1)}) fusion(f32[512,2560]{1,0:T(8,128)} %fusion.151, bf16[512,960]{0,1:T(8,128)(2,1)S(1)} %multiply_convert_fusion.12, bf16[960,2560]{1,0:T(8,128)(2,1)S(1)} %bitcast.135), kind=kOutput, calls=%fused_computation.36 | convolution fusion | flops 2525757440 | bytes 16384000 | tf_op jit(solution)/shard_map/kd,df->kf/dot_general | solution.py:27
  248.9 5.8 multiply_add_fusion.2
  255.2 2.6 fusion.104.qkv_ref
  260.8 11.7 %attend_fwd.5 = (bf16[256,960]{1,0:T(8,128)(2,1)}, bf16[15,256,64]{2,1,0:T(8,128)(2,1)}, bf16[5,256,64]{2,1,0:T(8,128)(2,1)}, bf16[5,256,64]{2,1,0:T(8,128)(2,1)}, f32[16,256]{1,0:T(8,128)}) custom-call(f32[256,1600]{1,0:T(8,128)} %fusion.104.qkv_ref, f32[256,64]{1,0:T(8,128)} %get-tuple-element.209.cos_ref, f32[256,64]{1,0:T(8,128)} %get-tuple-element.208.sin_ref, ...), custom_call_target="tpu_custom_call" | custom-call | tf_op jit(solution)/shard_map/attend_fwd/pallas_call | solution.py:78
  272.5 3.5 multiply_reduce_fusion.24
  277.9 3.0 multiply_convert_fusion.11
  283.2 3.2 multiply_reduce_fusion.23
  286.5 3.8 multiply_convert_fusion.9
  298.5 8.1 %attend_bwd.3 = bf16[256,1600]{1,0:T(8,128)(2,1)} custom-call(bf16[15,256,64]{2,1,0:T(8,128)(2,1)} %get-tuple-element.45.q_ref, bf16[5,256,64]{2,1,0:T(8,128)(2,1)} %get-tuple-element.46.k_ref, bf16[5,256,64]{2,1,0:T(8,128)(2,1)} %get-tuple-element.47.v_ref, f32[16,256]{1,0:T(8,128)} %get-tuple-element.48.lse_ref, bf16[256,960]{1,0:T(8,128)(2,1)} %copy.97.do_ref, ...), custom_call_target="tpu_custom_call" | custom-call | tf_op jit(solution)/shard_map/attend_bwd/pallas_call | solution.py:154
  306.5 4.0 multiply_reduce_fusion.20
  315.5 9.5 %multiply_convert_fusion.3 = (bf16[512,2560]{1,0:T(8,128)(2,1)S(1)}, bf16[512,2560]{1,0:T(8,128)(2,1)}) fusion(f32[512,2560]{1,0:T(8,128)} %fusion.151, bf16[512,2560]{1,0:T(8,128)(2,1)S(1)} %copy-done.94, bf16[512,960]{0,1:T(8,128)(2,1)S(1)} %get-tuple-element.171, bf16[2560,960]{1,0:T(8,128)(2,1)} %bitcast.149), kind=kOutput, calls=%fused_computation.34 | convolution fusion | flops 2536243200 | bytes 19005440 | tf_op jit(solution)/shard_map/kd,fd->kf/dot_general | solution.py:27
  325.1 5.4 fusion.154
  330.6 3.1 multiply_reduce_fusion.10
  340.3 19.9 %attend_bwd.4 = bf16[512,1600]{1,0:T(8,128)(2,1)} custom-call(bf16[15,512,64]{2,1,0:T(8,128)(2,1)} %get-tuple-element.49.q_ref, bf16[5,512,64]{2,1,0:T(8,128)(2,1)} %get-tuple-element.50.k_ref, bf16[5,512,64]{2,1,0:T(8,128)(2,1)} %get-tuple-element.51.v_ref, f32[16,512]{1,0:T(8,128)} %get-tuple-element.52.lse_ref, bf16[512,960]{1,0:T(8,128)(2,1)} %copy.98.do_ref, ...), custom_call_target="tpu_custom_call" | custom-call | tf_op jit(solution)/shard_map/attend_bwd/pallas_call | solution.py:154
  360.2 4.9 multiply_reduce_fusion.11
  368.1 13.6 %multiply_convert_fusion = (bf16[768,2560]{1,0:T(8,128)(2,1)S(1)}, bf16[768,2560]{1,0:T(8,128)(2,1)}) fusion(f32[768,2560]{1,0:T(8,128)} %copy-done.87, bf16[768,2560]{1,0:T(8,128)(2,1)} %get-tuple-element.183, bf16[768,960]{0,1:T(8,128)(2,1)S(1)} %get-tuple-element.165, bf16[2560,960]{1,0:T(8,128)(2,1)} %bitcast.150), kind=kOutput, calls=%fused_computation.23 | convolution fusion | flops 3804364800 | bytes 26050560 | tf_op jit(solution)/shard_map/kd,fd->kf/dot_general | solution.py:27
  381.7 7.5 %fusion.155 = f32[768,960]{0,1:T(8,128)S(1)} fusion(bf16[768,2560]{1,0:T(8,128)(2,1)} %get-tuple-element.156, bf16[960,2560]{1,0:T(8,128)(2,1)S(1)} %bitcast.105), kind=kOutput, calls=%fused_computation.280 | convolution fusion | flops 3774873600 | bytes 11796480 | tf_op jit(solution)/shard_map/kf,df->kd/dot_general | solution.py:27
  389.3 4.5 multiply_reduce_fusion.1
  395.5 2.8 convolution_convert_fusion
  400.9 36.4 %attend_bwd.5 = bf16[768,1600]{1,0:T(8,128)(2,1)} custom-call(bf16[15,768,64]{2,1,0:T(8,128)(2,1)} %get-tuple-element.53.q_ref, bf16[5,768,64]{2,1,0:T(8,128)(2,1)} %get-tuple-element.54.k_ref, bf16[5,768,64]{2,1,0:T(8,128)(2,1)} %get-tuple-element.55.v_ref, f32[16,768]{1,0:T(8,128)} %get-tuple-element.56.lse_ref, bf16[768,960]{1,0:T(8,128)(2,1)} %copy.99.do_ref, ...), custom_call_target="tpu_custom_call" | custom-call | tf_op jit(solution)/shard_map/attend_bwd/pallas_call | solution.py:154
  437.3 7.6 %multiply_reduce_fusion.2 = (f32[960]{0:T(1024)S(1)}, f32[768]{0:T(1024)S(1)}, f32[960]{0:T(1024)S(1)}, f32[768,960]{0,1:T(8,128)}) fusion(f32[1024,960]{0,1:T(8,128)S(1)} %copy-done.10, f32[768]{0:T(1024)S(1)} %copy-done.79, f32[960]{0:T(1024)S(1)} %mul.583, f32[768]{0:T(1024)S(1)} %subtract_multiply_fusion.3, bf16[768,1600]{1,0:T(8,128)(2,1)} %attend_bwd.5, ...), kind=kOutput, calls=%fused_computation.83 | convolution fusion | flops 2365191424 | bytes 11669760 | tf_op jit(solution)/shard_map/ke,de->kd/dot_general | solution.py:27
  445.6 11.9 %fusion.21 = bf16[2560,960]{0,1:T(8,128)(2,1)} fusion(bf16[768,2560]{1,0:T(8,128)(2,1)} %get-tuple-element.182, bf16[512,2560]{1,0:T(8,128)(2,1)} %get-tuple-element.187, bf16[256,2560]{1,0:T(8,128)(2,1)} %copy-done.55, bf16[768,960]{0,1:T(8,128)(2,1)S(1)} %copy-done.54, bf16[512,960]{0,1:T(8,128)(2,1)} %copy-done.60, ...), kind=kOutput, calls=%fused_computation.28 | convolution fusion | flops 7584645120 | bytes 15728640 | tf_op jit(solution)/shard_map/kd,ke->de/dot_general | solution.py:27
  457.5 8.0 %copy.100 = bf16[2560,960]{1,0:T(8,128)(2,1)} copy(bf16[2560,960]{0,1:T(8,128)(2,1)} %fusion.21) | data formatting | bytes 9830400 | tf_op jit(solution)/shard_map/convert_element_type | solution.py:777
  465.6 12.2 %fusion.24 = bf16[960,2560]{1,0:T(8,128)(2,1)} fusion(bf16[768,2560]{1,0:T(8,128)(2,1)} %copy-done.91, bf16[512,2560]{1,0:T(8,128)(2,1)} %copy-done.92, bf16[256,2560]{1,0:T(8,128)(2,1)} %copy-done.88, bf16[768,960]{0,1:T(8,128)(2,1)} %copy-done.51, bf16[512,960]{0,1:T(8,128)(2,1)S(1)} %copy-done.34, bf16[256,960]{0,1:T(8,128)(2,1)S(1)} %copy-done.41), kind=kOutput, calls=%fused_computation.29 | convolution fusion | flops 7584645120 | bytes 15728640 | tf_op jit(solution)/shard_map/kd,ke->de/dot_general | solution.py:27
  477.8 9.9 %fusion.27 = bf16[960,2560]{1,0:T(8,128)(2,1)} fusion(bf16[768,2560]{1,0:T(8,128)(2,1)S(1)} %copy-done.95, bf16[512,2560]{1,0:T(8,128)(2,1)S(1)} %copy-done.93, bf16[256,2560]{1,0:T(8,128)(2,1)S(1)} %copy-done.90, bf16[768,960]{0,1:T(8,128)(2,1)S(1)} %copy-done.52, bf16[512,960]{0,1:T(8,128)(2,1)S(1)} %copy-done.34, bf16[256,960]{0,1:T(8,128)(2,1)S(1)} %copy-done.41), kind=kOutput, calls=%fused_computation.30 | convolution fusion | flops 7584645120 | bytes 15728640 | tf_op jit(solution)/shard_map/kd,ke->de/dot_general | solution.py:27
  487.9 3.6 fusion.87
  491.6 5.5 fusion.44
  497.1 4.0 pad_maximum_fusion
  501.1 167.5 %reduce_grads.1 = (bf16[2,120,2560]{2,1,0:T(8,128)(2,1)}, bf16[2,120,2560]{2,1,0:T(8,128)(2,1)}, bf16[2,120,2560]{2,1,0:T(8,128)(2,1)}, bf16[2,320,960]{2,1,0:T(8,128)(2,1)}, f32[8,1024]{1,0:T(8,128)}) custom-call(bf16[4,2,120,2560]{3,2,1,0:T(8,128)(2,1)} %bitcast.147, bf16[4,2,120,2560]{3,2,1,0:T(8,128)(2,1)} %bitcast.159, ...), custom_call_target="tpu_custom_call" | custom-call | tf_op jit(solution)/shard_map/reduce_grads/pallas_call | solution.py:662
  668.6 3.1 bitcast_convert_fusion
  671.7 3.3 copy.103
  678.9 3.2 bitcast_convert_fusion.1
  682.0 3.0 bitcast_convert_fusion.2
  687.8 5.3 add_convert_fusion
  694.4 3.6 fusion.95
  701.8 3.5 fusion.92
  (357 shorter events, 79.1 us)
Async XLA Ops:
  4.3 276.6 %copy-start.85 = (s32[1024]{0:T(1024)}, s32[1024]{0:T(1024)S(1)}, u32[]{:S(2)}) copy-start(s32[1024]{0:T(1024)S(1)} %fusion.113) | copy-start | bytes 12292
  113.0 10.5 %copy-start.78 = (f32[768]{0:T(1024)}, f32[768]{0:T(1024)S(1)}, u32[]{:S(2)}) copy-start(f32[768]{0:T(1024)S(1)} %get-tuple-element.202) | copy-start | bytes 9220
  126.7 78.1 %copy-start.27 = (f32[1024,32]{1,0:T(8,128)}, f32[1024,32]{1,0:T(8,128)S(1)}, u32[]{:S(2)}) copy-start(f32[1024,32]{1,0:T(8,128)S(1)} %get-tuple-element.180) | copy-start | bytes 393220
  128.8 36.9 %copy-start.42 = (f32[1024,2]{1,0:T(8,128)}, f32[1024,2]{1,0:T(8,128)S(1)}, u32[]{:S(2)}) copy-start(f32[1024,2]{1,0:T(8,128)S(1)} %convert_element_type.222) | copy-start | bytes 24580
  129.6 36.1 %copy-start.8 = (f32[1024,960]{0,1:T(8,128)S(1)}, f32[1024,960]{0,1:T(8,128)}, u32[]{:S(2)}) copy-start(f32[1024,960]{0,1:T(8,128)} %fusion.42) | copy-start | bytes 11796484
  172.0 9.4 %copy-start.72 = (f32[768]{0:T(1024)}, f32[768]{0:T(1024)S(1)}, u32[]{:S(2)}) copy-start(f32[768]{0:T(1024)S(1)} %add_rsqrt_fusion) | copy-start | bytes 9220
  172.1 9.3 %slice-start.14 = ((s8[4915200]{0:T(1024)(128)(4,1)}), s8[4194304]{0:T(1024)(128)(4,1)S(1)}, s32[]{:S(2)}) async-start(s8[4915200]{0:T(1024)(128)(4,1)} %bitcast.130), calls=%async_computation.14 | async-start | bytes 8388608
  189.3 11.5 %slice-start.6 = ((s8[4915200]{0:T(1024)(128)(4,1)}), s8[4194304]{0:T(1024)(128)(4,1)S(1)}, s32[]{:S(2)}) async-start(s8[4915200]{0:T(1024)(128)(4,1)} %bitcast.114), calls=%async_computation.6 | async-start | bytes 8388608
  189.3 11.5 %slice-start.7 = ((s8[4915200]{0:T(1024)(128)(4,1)}), s8[720896]{0:T(1024)(128)(4,1)S(1)}, s32[]{:S(2)}) async-start(s8[4915200]{0:T(1024)(128)(4,1)} %bitcast.114), calls=%async_computation.7 | async-start | bytes 1441792
  232.6 9.0 %slice-start.16 = ((s8[4915200]{0:T(1024)(128)(4,1)}), s8[4194304]{0:T(1024)(128)(4,1)S(1)}, s32[]{:S(2)}) async-start(s8[4915200]{0:T(1024)(128)(4,1)} %bitcast.133), calls=%async_computation.16 | async-start | bytes 8388608
  236.7 12.2 %slice-start.24 = ((s8[5242880]{0:T(1024)(128)(4,1)}), s8[4194304]{0:T(1024)(128)(4,1)S(1)}, s32[]{:S(2)}) async-start(s8[5242880]{0:T(1024)(128)(4,1)} %bitcast.151), calls=%async_computation.24 | async-start | bytes 8388608
  236.8 18.4 %slice-start.8 = ((s8[4915200]{0:T(1024)(128)(4,1)}), s8[4194304]{0:T(1024)(128)(4,1)S(1)}, s32[]{:S(2)}) async-start(s8[4915200]{0:T(1024)(128)(4,1)} %bitcast.117), calls=%async_computation.8 | async-start | bytes 8388608
  241.5 13.6 %slice-start.9 = ((s8[4915200]{0:T(1024)(128)(4,1)}), s8[720896]{0:T(1024)(128)(4,1)S(1)}, s32[]{:S(2)}) async-start(s8[4915200]{0:T(1024)(128)(4,1)} %bitcast.117), calls=%async_computation.9 | async-start | bytes 1441792
  276.0 17.5 %copy-start.20 = (f32[256,960]{0,1:T(8,128)}, f32[256,960]{0,1:T(8,128)S(1)}, u32[]{:S(2)}) copy-start(f32[256,960]{0,1:T(8,128)S(1)} %get-tuple-element.150) | copy-start | bytes 2949124
  283.2 10.3 %copy-start.23 = (f32[1024,960]{0,1:T(8,128)}, f32[1024,960]{0,1:T(8,128)S(1)}, u32[]{:S(2)}) copy-start(f32[1024,960]{0,1:T(8,128)S(1)} %fusion.40) | copy-start | bytes 11796484
  298.5 8.1 %copy-start.26 = (f32[512,960]{0,1:T(8,128)S(1)}, f32[512,960]{0,1:T(8,128)}, u32[]{:S(2)}) copy-start(f32[512,960]{0,1:T(8,128)} %copy-done.25) | copy-start | bytes 5898244
  310.7 19.8 %slice-start.20 = ((s8[4915200]{0:T(1024)(128)(4,1)}), s8[4194304]{0:T(1024)(128)(4,1)S(1)}, s32[]{:S(2)}) async-start(s8[4915200]{0:T(1024)(128)(4,1)} %bitcast.140), calls=%async_computation.20 | async-start | bytes 8388608
  312.6 21.1 %copy-start.16 = (f32[256,960]{0,1:T(8,128)}, f32[256,960]{0,1:T(8,128)S(1)}, u32[]{:S(2)}) copy-start(f32[256,960]{0,1:T(8,128)S(1)} %get-tuple-element.163) | copy-start | bytes 2949124
  312.6 12.4 %slice-start.2 = ((s8[4915200]{0:T(1024)(128)(4,1)}), s8[4194304]{0:T(1024)(128)(4,1)S(1)}, s32[]{:S(2)}) async-start(s8[4915200]{0:T(1024)(128)(4,1)} %bitcast.100), calls=%async_computation.2 | async-start | bytes 8388608
  313.1 11.9 %copy-start.60 = (bf16[512,960]{0,1:T(8,128)(2,1)}, bf16[512,960]{0,1:T(8,128)(2,1)S(1)}, u32[]{:S(2)}) copy-start(bf16[512,960]{0,1:T(8,128)(2,1)S(1)} %get-tuple-element.171) | copy-start | bytes 2949124
  315.5 9.5 %slice-start.3 = ((s8[4915200]{0:T(1024)(128)(4,1)}), s8[720896]{0:T(1024)(128)(4,1)S(1)}, s32[]{:S(2)}) async-start(s8[4915200]{0:T(1024)(128)(4,1)} %bitcast.100), calls=%async_computation.3 | async-start | bytes 1441792
  315.5 15.0 %slice-start.21 = ((s8[4915200]{0:T(1024)(128)(4,1)}), s8[720896]{0:T(1024)(128)(4,1)S(1)}, s32[]{:S(2)}) async-start(s8[4915200]{0:T(1024)(128)(4,1)} %bitcast.140), calls=%async_computation.21 | async-start | bytes 1441792
  325.1 10.8 %slice-start.10 = ((s8[4915200]{0:T(1024)(128)(4,1)}), s8[4194304]{0:T(1024)(128)(4,1)S(1)}, s32[]{:S(2)}) async-start(s8[4915200]{0:T(1024)(128)(4,1)} %bitcast.120), calls=%async_computation.10 | async-start | bytes 8388608
  340.3 19.9 %copy-start.15 = (f32[768,960]{0,1:T(8,128)S(1)}, f32[768,960]{0,1:T(8,128)}, u32[]{:S(2)}) copy-start(f32[768,960]{0,1:T(8,128)} %copy-done.13) | copy-start | bytes 8847364
  366.4 27.4 %copy-start.11 = (f32[512,960]{0,1:T(8,128)}, f32[512,960]{0,1:T(8,128)S(1)}, u32[]{:S(2)}) copy-start(f32[512,960]{0,1:T(8,128)S(1)} %multiply_add_fusion.1) | copy-start | bytes 5898244
  367.3 14.4 %slice-start.4 = ((s8[4915200]{0:T(1024)(128)(4,1)}), s8[4194304]{0:T(1024)(128)(4,1)S(1)}, s32[]{:S(2)}) async-start(s8[4915200]{0:T(1024)(128)(4,1)} %bitcast.103), calls=%async_computation.4 | async-start | bytes 8388608
  367.3 22.0 %slice-start.22 = ((s8[4915200]{0:T(1024)(128)(4,1)}), s8[4194304]{0:T(1024)(128)(4,1)S(1)}, s32[]{:S(2)}) async-start(s8[4915200]{0:T(1024)(128)(4,1)} %bitcast.143), calls=%async_computation.22 | async-start | bytes 8388608
  368.0 13.6 %copy-start.53 = (bf16[768,960]{0,1:T(8,128)(2,1)}, bf16[768,960]{0,1:T(8,128)(2,1)S(1)}, u32[]{:S(2)}) copy-start(bf16[768,960]{0,1:T(8,128)(2,1)S(1)} %get-tuple-element.165) | copy-start | bytes 4423684
  368.0 13.6 %slice-start.5 = ((s8[4915200]{0:T(1024)(128)(4,1)}), s8[720896]{0:T(1024)(128)(4,1)S(1)}, s32[]{:S(2)}) async-start(s8[4915200]{0:T(1024)(128)(4,1)} %bitcast.103), calls=%async_computation.5 | async-start | bytes 1441792
  368.0 21.2 %slice-start.23 = ((s8[4915200]{0:T(1024)(128)(4,1)}), s8[720896]{0:T(1024)(128)(4,1)S(1)}, s32[]{:S(2)}) async-start(s8[4915200]{0:T(1024)(128)(4,1)} %bitcast.143), calls=%async_computation.23 | async-start | bytes 1441792
  381.7 13.8 %slice-start.12 = ((s8[4915200]{0:T(1024)(128)(4,1)}), s8[4194304]{0:T(1024)(128)(4,1)S(1)}, s32[]{:S(2)}) async-start(s8[4915200]{0:T(1024)(128)(4,1)} %bitcast.123), calls=%async_computation.12 | async-start | bytes 8388608
  400.9 36.4 %copy-start.75 = (f32[768]{0:T(1024)S(1)}, f32[768]{0:T(1024)}, u32[]{:S(2)}) copy-start(f32[768]{0:T(1024)} %copy-done.74) | copy-start | bytes 9220
  400.9 36.4 %copy-start.10 = (f32[1024,960]{0,1:T(8,128)S(1)}, f32[1024,960]{0,1:T(8,128)}, u32[]{:S(2)}) copy-start(f32[1024,960]{0,1:T(8,128)} %fusion.42) | copy-start | bytes 11796484
  400.9 36.4 %copy-start.79 = (f32[768]{0:T(1024)S(1)}, f32[768]{0:T(1024)}, u32[]{:S(2)}) copy-start(f32[768]{0:T(1024)} %copy-done.78) | copy-start | bytes 9220
  437.3 8.3 %copy-start.54 = (bf16[768,960]{0,1:T(8,128)(2,1)S(1)}, bf16[768,960]{0,1:T(8,128)(2,1)}, u32[]{:S(2)}) copy-start(bf16[768,960]{0,1:T(8,128)(2,1)} %copy-done.53) | copy-start | bytes 4423684
  457.5 8.0 %copy-start.41 = (bf16[256,960]{0,1:T(8,128)(2,1)S(1)}, bf16[256,960]{0,1:T(8,128)(2,1)}, u32[]{:S(2)}) copy-start(bf16[256,960]{0,1:T(8,128)(2,1)} %copy-done.40) | copy-start | bytes 1474564
  465.5 12.2 %copy-start.52 = (bf16[768,960]{0,1:T(8,128)(2,1)S(1)}, bf16[768,960]{0,1:T(8,128)(2,1)}, u32[]{:S(2)}) copy-start(bf16[768,960]{0,1:T(8,128)(2,1)} %copy-done.51) | copy-start | bytes 4423684
  465.5 12.2 %copy-start.90 = (bf16[256,2560]{1,0:T(8,128)(2,1)S(1)}, bf16[256,2560]{1,0:T(8,128)(2,1)}, u32[]{:S(2)}) copy-start(bf16[256,2560]{1,0:T(8,128)(2,1)} %copy-done.89) | copy-start | bytes 3932164
  465.5 12.2 %copy-start.93 = (bf16[512,2560]{1,0:T(8,128)(2,1)S(1)}, bf16[512,2560]{1,0:T(8,128)(2,1)}, u32[]{:S(2)}) copy-start(bf16[512,2560]{1,0:T(8,128)(2,1)} %get-tuple-element.158) | copy-start | bytes 7864324
  465.6 12.2 %copy-start.95 = (bf16[768,2560]{1,0:T(8,128)(2,1)S(1)}, bf16[768,2560]{1,0:T(8,128)(2,1)}, u32[]{:S(2)}) copy-start(bf16[768,2560]{1,0:T(8,128)(2,1)} %get-tuple-element.156) | copy-start | bytes 11796484
  477.8 10.0 %copy-start.48 = (bf16[768,960]{1,0:T(8,128)(2,1)S(1)}, bf16[768,960]{1,0:T(8,128)(2,1)}, u32[]{:S(2)}) copy-start(bf16[768,960]{1,0:T(8,128)(2,1)} %get-tuple-element.39) | copy-start | bytes 4423684
  477.8 10.0 %copy-start.50 = (bf16[768,960]{0,1:T(8,128)(2,1)S(1)}, bf16[768,960]{0,1:T(8,128)(2,1)}, u32[]{:S(2)}) copy-start(bf16[768,960]{0,1:T(8,128)(2,1)} %copy-done.49) | copy-start | bytes 4423684
  477.8 10.0 %copy-start.57 = (bf16[512,960]{1,0:T(8,128)(2,1)S(1)}, bf16[512,960]{1,0:T(8,128)(2,1)}, u32[]{:S(2)}) copy-start(bf16[512,960]{1,0:T(8,128)(2,1)} %get-tuple-element.43) | copy-start | bytes 2949124
  477.8 10.0 %copy-start.59 = (bf16[512,960]{0,1:T(8,128)(2,1)S(1)}, bf16[512,960]{0,1:T(8,128)(2,1)}, u32[]{:S(2)}) copy-start(bf16[512,960]{0,1:T(8,128)(2,1)} %copy-done.58) | copy-start | bytes 2949124
  477.8 10.0 %copy-start.62 = (bf16[256,960]{1,0:T(8,128)(2,1)S(1)}, bf16[256,960]{1,0:T(8,128)(2,1)}, u32[]{:S(2)}) copy-start(bf16[256,960]{1,0:T(8,128)(2,1)} %get-tuple-element.44) | copy-start | bytes 1474564
  477.8 10.0 %copy-start.69 = (bf16[256,960]{0,1:T(8,128)(2,1)S(1)}, bf16[256,960]{0,1:T(8,128)(2,1)}, u32[]{:S(2)}) copy-start(bf16[256,960]{0,1:T(8,128)(2,1)} %copy-done.68) | copy-start | bytes 1474564
  678.9 9.0 %copy-start.12 = (f32[512,960]{0,1:T(8,128)S(1)}, f32[512,960]{0,1:T(8,128)}, u32[]{:S(2)}) copy-start(f32[512,960]{0,1:T(8,128)} %copy-done.11) | copy-start | bytes 5898244
  678.9 9.0 %copy-start.77 = (f32[960,1]{0,1:T(1,128)S(1)}, f32[960,1]{0,1:T(1,128)}, u32[]{:S(2)}) copy-start(f32[960,1]{0,1:T(1,128)} %copy-done.76) | copy-start | bytes 11524
  (76 other events, 306.5 us)

commit v3 on v2

--- a/solution.py
+++ b/solution.py
@@ -39,40 +39,60 @@
 KW = KV_HEADS * HEAD_DIM
 
 
-def attend_fwd_kernel(qkv_ref, cos_ref, sin_ref, cols_ref, rows_ref, o_ref, q_ref, k_ref, v_ref, lse_ref, bias, stats):
+def attend_fwd_kernel(
+    qkv_ref, cos_ref, sin_ref, cols_ref, rows_ref, o_ref, q_ref, k_ref, v_ref, lse_ref, bias, vt
+):
     step = pl.program_id(0)
-    rows = pl.ds(pl.multiple_of(step * ROWS, ROWS), ROWS)
+    start = pl.multiple_of(step * ROWS, ROWS)
+    rows = pl.ds(start, ROWS)
+
+    def turned(at, column, cos, sin):
+        raw = qkv_ref[at, column : column + 128]
+        lane = lax.broadcasted_iota(jnp.int32, raw.shape, 1)
+        swapped = jnp.where(lax.rem(lane, HEAD_DIM) < HALF, pltpu.roll(raw, 128 - HALF, 1), pltpu.roll(raw, HALF, 1))
+        return raw * cos + swapped * sin
 
     @pl.when(step == 0)
     def _():
+        everything = slice(None)
         cos, sin = cos_ref[...], sin_ref[...]
+        for column in range(QW // 128 * 128, QW + KW, 128):
+            keys = turned(everything, column, cos, sin).astype(bf16)
+            for part in range(2):
+                g = (column + part * HEAD_DIM - QW) // HEAD_DIM
+                if 0 <= g < KV_HEADS:
+                    k_ref[g] = keys[:, part * HEAD_DIM : (part + 1) * HEAD_DIM]
         for g in range(KV_HEADS):
-            raw = qkv_ref[:, QW + g * HEAD_DIM : QW + (g + 1) * HEAD_DIM]
-            k_ref[g] = (raw * cos + swap_halves(raw) * sin).astype(bf16)
-            v_ref[g] = qkv_ref[:, QW + KW + g * HEAD_DIM : QW + KW + (g + 1) * HEAD_DIM].astype(bf16)
-
-    cols = cols_ref[rows, :]
-    token, begin = cols[:, 0:1], cols[:, 1:2]
-    key_token = rows_ref[0:1, :]
+            value = qkv_ref[:, QW + KW + g * HEAD_DIM : QW + KW + (g + 1) * HEAD_DIM]
+            v_ref[g] = value.astype(bf16)
+            vt[g] = jnp.transpose(value).astype(bf16)
+
+    key_token = cols_ref[:, 0:1]
+    token, begin = rows_ref[0:1, pl.ds(start, ROWS)], rows_ref[1:2, pl.ds(start, ROWS)]
     bias[...] = jnp.where((key_token <= token) & (key_token >= begin), 0.0, masked_score)
-    cos, sin = cos_ref[rows, :], sin_ref[rows, :]
-    stats[...] = jnp.zeros_like(stats)
-    for n in range(HEADS):
-        g = n // GROUP
-        raw = qkv_ref[rows, n * HEAD_DIM : (n + 1) * HEAD_DIM]
-        q = ((raw * cos + swap_halves(raw) * sin).astype(bf16).astype(f32) * (1.0 / math.sqrt(HEAD_DIM))).astype(bf16)
-        q_ref[n, rows, :] = q
-        s = matmul(q, k_ref[g], ((1,), (1,))) + bias[...]
-        m = jnp.max(s, axis=1, keepdims=True)
-        p = jnp.exp(s - m)
-        t = jnp.sum(p, axis=1, keepdims=True)
-        p = (p * (1.0 / t)).astype(bf16)
-        o_ref[rows, n * HEAD_DIM : (n + 1) * HEAD_DIM] = matmul(p, v_ref[g], ((1,), (0,))).astype(bf16)
-        stats[:, n : n + 1] = m + jnp.log(t)
-    lse_ref[...] = jnp.transpose(stats[...])[:16]
-
-
-def attend_fwd(qkv, cos, sin, cols, rows):
+    scale = 1.0 / math.sqrt(HEAD_DIM)
+    cos, sin = cos_ref[rows, :] * scale, sin_ref[rows, :] * scale
+    for first in range(0, HEADS, 2):
+        pair = turned(rows, first * HEAD_DIM, cos, sin).astype(bf16)
+        outs = []
+        for n in range(first, min(first + 2, HEADS)):
+            g = n // GROUP
+            q = pair[:, (n - first) * HEAD_DIM : (n - first + 1) * HEAD_DIM]
+            q_ref[n, rows, :] = q
+            s = matmul(k_ref[g], q, ((1,), (1,))) + bias[...]
+            m = jnp.max(s, axis=0, keepdims=True)
+            p = jnp.exp(s - m)
+            t = jnp.sum(p, axis=0, keepdims=True)
+            p = (p * (1.0 / t)).astype(bf16)
+            outs.append(matmul(vt[g], p, ((1,), (0,))))
+            lse_ref[n : n + 1, :] = m + jnp.log(t)
+        width = HEAD_DIM * len(outs)
+        o_ref[rows, first * HEAD_DIM : first * HEAD_DIM + width] = jnp.transpose(jnp.concatenate(outs, axis=0)).astype(
+            bf16
+        )
+
+
+def attend_fwd(qkv, cos, sin, cos_t, sin_t, cols, rows):
     k = qkv.shape[0]
     whole = lambda *shape: pl.BlockSpec(shape, lambda i: (0,) * len(shape))
     return pl.pallas_call(
@@ -87,8 +107,8 @@
         ),
         in_specs=[
             whole(k, QW + 2 * KW),
-            whole(k, HEAD_DIM),
-            whole(k, HEAD_DIM),
+            whole(k, 2 * HEAD_DIM),
+            whole(k, 2 * HEAD_DIM),
             whole(k, 2),
             whole(2, k),
         ],
@@ -99,14 +119,15 @@
             whole(KV_HEADS, k, HEAD_DIM),
             pl.BlockSpec((16, ROWS), lambda i: (0, i)),
         ),
-        scratch_shapes=[pltpu.VMEM((ROWS, k), f32), pltpu.VMEM((ROWS, 128), f32)],
+        scratch_shapes=[pltpu.VMEM((k, ROWS), f32), pltpu.VMEM((KV_HEADS, HEAD_DIM, k), bf16)],
         compiler_params=pltpu.CompilerParams(vmem_limit_bytes=56 << 20),
         name="attend_fwd",
     )(qkv, cos, sin, cols, rows)
 
 
 def attend_bwd_kernel(
-    q_ref, k_ref, v_ref, lse_ref, do_ref, cos_ref, sin_ref, cols_ref, rows_ref, out_ref, bias, dk, dv, kt
+    q_ref, k_ref, v_ref, lse_ref, do_ref, cos_ref, sin_ref, cos_t_ref, sin_t_ref, cols_ref, rows_ref, out_ref,
+    bias, dk, dv, kt,
 ):
     step = pl.program_id(0)
     start = pl.multiple_of(step * ROWS, ROWS)
@@ -122,24 +143,32 @@
     key_token = cols_ref[:, 0:1]
     token, begin = rows_ref[0:1, pl.ds(start, ROWS)], rows_ref[1:2, pl.ds(start, ROWS)]
     bias[...] = jnp.where((key_token <= token) & (key_token >= begin), 0.0, masked_score)
-    cos, sin = cos_ref[rows, :], sin_ref[rows, :]
-    for n in range(HEADS):
-        g = n // GROUP
-        q = q_ref[n, rows, :]
-        do = do_ref[rows, n * HEAD_DIM : (n + 1) * HEAD_DIM]
-        s = matmul(k_ref[g], q, ((1,), (1,))) + bias[...]
-        p = jnp.exp(s - lse_ref[n : n + 1, :])
-        dp = matmul(v_ref[g], do, ((1,), (1,)))
-        dv[g] += matmul(p.astype(bf16), do, ((1,), (0,)))
-        pd = p * dp
-        ds = (pd - p * jnp.sum(pd, axis=0, keepdims=True)).astype(bf16)
-        dk[g] += matmul(ds, q, ((1,), (0,)))
-        dq = jnp.transpose(matmul(kt[g], ds, ((1,), (0,)))) * (1.0 / math.sqrt(HEAD_DIM))
-        out_ref[rows, n * HEAD_DIM : (n + 1) * HEAD_DIM] = (dq * cos - swap_halves(dq) * sin).astype(bf16)
+    scale = 1.0 / math.sqrt(HEAD_DIM)
+    cos, sin = cos_t_ref[...] * scale, sin_t_ref[...] * scale
+    for first in range(0, HEADS, 2):
+        count = min(2, HEADS - first)
+        grads = do_ref[rows, first * HEAD_DIM : (first + count) * HEAD_DIM]
+        outs = []
+        for n in range(first, first + count):
+            g = n // GROUP
+            q = q_ref[n, rows, :]
+            do = grads[:, (n - first) * HEAD_DIM : (n - first + 1) * HEAD_DIM]
+            s = matmul(k_ref[g], q, ((1,), (1,))) + bias[...]
+            p = jnp.exp(s - lse_ref[n : n + 1, :])
+            dp = matmul(v_ref[g], do, ((1,), (1,)))
+            dv[g] += matmul(p.astype(bf16), do, ((1,), (0,)))
+            pd = p * dp
+            ds = (pd - p * jnp.sum(pd, axis=0, keepdims=True)).astype(bf16)
+            dk[g] += matmul(ds, q, ((1,), (0,)))
+            dq = matmul(kt[g], ds, ((1,), (0,)))
+            outs.append(dq * cos - jnp.concatenate([dq[HALF:], dq[:HALF]], axis=0) * sin)
+        out_ref[rows, first * HEAD_DIM : (first + count) * HEAD_DIM] = jnp.transpose(
+            jnp.concatenate(outs, axis=0)
+        ).astype(bf16)
 
     @pl.when(step == pl.num_programs(0) - 1)
     def _():
-        cos, sin = cos_ref[...], sin_ref[...]
+        cos, sin = cos_ref[:, :HEAD_DIM], sin_ref[:, :HEAD_DIM]
         for g in range(KV_HEADS):
             grad = dk[g]
             out_ref[:, QW + g * HEAD_DIM : QW + (g + 1) * HEAD_DIM] = (
@@ -148,7 +177,7 @@
             out_ref[:, QW + KW + g * HEAD_DIM : QW + KW + (g + 1) * HEAD_DIM] = dv[g].astype(bf16)
 
 
-def attend_bwd(q, k, v, lse, grad, cos, sin, cols, rows):
+def attend_bwd(q, k, v, lse, grad, cos, sin, cos_t, sin_t, cols, rows):
     count = grad.shape[0]
     whole = lambda *shape: pl.BlockSpec(shape, lambda i: (0,) * len(shape))
     return pl.pallas_call(
@@ -161,8 +190,10 @@
             whole(KV_HEADS, count, HEAD_DIM),
             pl.BlockSpec((16, ROWS), lambda i: (0, i)),
             whole(count, QW),
-            whole(count, HEAD_DIM),
-            whole(count, HEAD_DIM),
+            whole(count, 2 * HEAD_DIM),
+            whole(count, 2 * HEAD_DIM),
+            pl.BlockSpec((HEAD_DIM, ROWS), lambda i: (0, i)),
+            pl.BlockSpec((HEAD_DIM, ROWS), lambda i: (0, i)),
             whole(count, 2),
             whole(2, count),
         ],
@@ -175,7 +206,7 @@
         ],
         compiler_params=pltpu.CompilerParams(vmem_limit_bytes=56 << 20),
         name="attend_bwd",
-    )(q, k, v, lse, grad, cos, sin, cols, rows)
+    )(q, k, v, lse, grad, cos, sin, cos_t, sin_t, cols, rows)
 
 
 def inverse_rms(values):
@@ -539,55 +570,57 @@
                 def _():
                     down_copy(a, t).start()
 
-    def stage5(t):
+    def stage5(t, level):
         for a in range(4):
-            if t > 0:
-
-                @pl.when((z > 0) & (z <= t))
-                def _():
-                    up_copy(a, t).wait_recv()
-                    add_piece(a, t, up[a], own_index(a), 4)
-
-                @pl.when((z > 0) & (z < t))
-                def _():
+            if 0 < level <= t:
+                up_copy(a, t).wait_recv()
+                add_piece(a, t, up[a], own_index(a), 4)
+                if level < t:
                     up_copy(a, t).start()
-
-            if t < 3:
-
-                @pl.when((z < 3) & (z >= t))
-                def _():
-                    down_copy(a, t).wait_recv()
-                    add_piece(a, t, down[a], own_index(a), 4)
-
-                @pl.when((z < 3) & (z > t))
-                def _():
+            if t <= level < 3:
+                down_copy(a, t).wait_recv()
+                add_piece(a, t, down[a], own_index(a), 4)
+                if level > t:
                     down_copy(a, t).start()
 
     def small_copy(k, name):
         return remote(small_out_buf.at[k], small_in.at[k], ssend.at[k], srecv.at[k], ids[name])
 
+    def small_step(k, name):
+        small_copy(k, name).wait_recv()
+        small_out[...] = small_out[...] + small_in[k]
+
+    def small_send(k, name):
+        small_out_buf[k] = small_out[...]
+        small_copy(k, name).start()
+
+    small_out[...] = small[...]
+    small_send(0, "core")
     for t in TARGETS:
         for a in range(4):
             core_copy(a, t).start()
             load(a, t).start()
-    total = small[...]
-    for k, name in enumerate(("core", "x", "y")):
-        small_out_buf[k] = total
-        small_copy(k, name).start()
-        small_copy(k, name).wait_recv()
-        total = total + small_in[k]
-    small_out[...] = total
+    small_step(0, "core")
+    small_send(1, "x")
+    small_step(1, "x")
+    small_send(2, "y")
 
     n = len(TARGETS)
-    for k in range(n + 3):
+    turns = {3: [(3, 1)], 4: [(3, 2), (0, 2)], 5: [(3, 3), (0, 1), (2, 1)], 6: [(0, 0), (2, 2), (1, 2)], 7: [(1, 1)]}
+    for k in range(n + 4):
         if k < n:
             stage2(TARGETS[k])
         if 1 <= k < n + 1:
             stage3(TARGETS[k - 1])
         if 2 <= k < n + 2:
             stage4(TARGETS[k - 2])
-        if 3 <= k:
-            stage5(TARGETS[k - 3])
+        for t, level in turns.get(k, ()):
+
+            @pl.when(z == level)
+            def _():
+                stage5(t, level)
+
+    small_step(2, "y")
 
     small_out_buf[3] = small_out[...]
     small_out_buf[4] = small_out[...]
@@ -732,11 +765,12 @@
     frequency = jnp.exp(jnp.arange(HALF, dtype=f32) * (-2.0 * math.log(10000.0) / HEAD_DIM))
     angles = (token - begin).astype(f32)[:, None] * frequency[None, :]
     cos, sin = jnp.cos(angles), jnp.sin(angles)
-    cos = jnp.concatenate([cos, cos], axis=1)
-    sin = jnp.concatenate([-sin, sin], axis=1)
+    cos = jnp.concatenate([cos] * 4, axis=1)
+    sin = jnp.concatenate([-sin, sin] * 2, axis=1)
+    cos_t, sin_t = cos[:, :HEAD_DIM].T, sin[:, :HEAD_DIM].T
     rows2 = jnp.stack([token, begin]).astype(f32)
     cols2 = jnp.stack([token, begin], axis=1).astype(f32)
-    tables = [(cos[:k], sin[:k], cols2[:k], rows2[:, :k]) for k in counts]
+    tables = [(cos[:k], sin[:k], cos_t[:, :k], sin_t[:, :k], cols2[:k], rows2[:, :k]) for k in counts]
 
     hidden = dot("pt,td->pd", order, inputs)
     grads = dot("pt,td->pd", order, out_grad)

time: 711 us -> 693 us (0.975)
  Pallas kernels: 395 us -> 378 us
  local copies, waits for them, and re-layouts: 53.8 us -> 63.1 us
    slice x5 -> x21, local copies, waits for them, and re-layouts: 4.31 us -> 14.2 us  [the longest x5 3.48 us: body(): cos[:k]]
    pallas_call x3, Pallas kernels: 73.2 us -> 64.2 us  [attend_fwd(): pl.pallas_call(attend_fwd_kernel, grid=(k // ROWS,), out_shape=(jax.Shape...]
    unnamed x254 -> x272, local copies, waits for them, and re-layouts: 24.1 us -> 23.4 us
where the time goes in v3:
time: 693 us; the launch traced here: 688 us
  Pallas kernels  378 us (55%)
  matrix products  203 us (29%)
  local copies, waits for them, and re-layouts  63.1 us (9%)
  other arithmetic  40.1 us (6%)
    dot_general x40, matrix products, dot(): return jnp.einsum(spec, left, right, preferred_element_type=f32)  203 us
    pallas_call x1, Pallas kernels, reduce_grads(): pl.pallas_call(reduce_kernel, out_shape=tuple((jax.ShapeDtypeStruct(g.sha...  161 us
    pallas_call x1, Pallas kernels, gather_weights(): pl.pallas_call(gather_kernel, out_shape=tuple((jax.ShapeDtypeStruct((4, *...  90 us
    pallas_call x3, Pallas kernels, attend_fwd(): pl.pallas_call(attend_fwd_kernel, grid=(k // ROWS,), out_shape=(jax.Shape...  64.2 us
    pallas_call x3, Pallas kernels, attend_bwd(): pl.pallas_call(attend_bwd_kernel, grid=(count // ROWS,), out_shape=jax.Sh...  63.4 us
    unnamed x272, local copies, waits for them, and re-layouts  23.4 us

profile of v3, /device:TPU:0, one launch (start us, length us, event | category | flops | bytes accessed | tf_op | source)
XLA Modules:
  0.0 687.8 jit_solution(7586774184249819917)
XLA Ops:
  4.3 4.3 fusion.42
  14.0 90.0 %gather_weights.1 = (bf16[4,2,120,2560]{3,2,1,0:T(8,128)(2,1)S(1)}, bf16[4,2,120,2560]{3,2,1,0:T(8,128)(2,1)S(1)}, bf16[4,2,120,2560]{3,2,1,0:T(8,128)(2,1)S(1)}...) custom-call(bf16[2,120,2560]{2,1,0:T(8,128)(2,1)S(1)} %bitcast.133, bf16[2,120,2560]{2,1,0:T(8,128)(2,1)S(1)} %bitcast.134, ...), custom_call_target="tpu_custom_call" | custom-call | tf_op jit(solution)/shard_map/gather_weights/pallas_call | solution.py:454
  115.8 7.7 %fusion.108.qkv_ref = f32[768,1600]{1,0:T(8,128)} fusion(bf16[768,960]{0,1:T(8,128)(2,1)S(1)} %multiply_convert_fusion.7, bf16[960,2560]{1,0:T(8,128)(2,1)} %bitcast.112), kind=kOutput, calls=%fused_computation.157 | convolution fusion | flops 2359296000 | bytes 9584640 | tf_op jit(solution)/shard_map/kd,de->ke/dot_general | solution.py:27
  129.1 36.2 %attend_fwd.3 = (bf16[768,960]{1,0:T(8,128)(2,1)}, bf16[15,768,64]{2,1,0:T(8,128)(2,1)}, bf16[5,768,64]{2,1,0:T(8,128)(2,1)}, bf16[5,768,64]{2,1,0:T(8,128)(2,1)}, f32[16,768]{1,0:T(8,128)}) custom-call(f32[768,1600]{1,0:T(8,128)} %fusion.108.qkv_ref, f32[768,128]{1,0:T(8,128)} %copy.142.cos_ref, f32[768,128]{1,0:T(8,128)} %copy.143.sin_ref, ...), custom_call_target="tpu_custom_call" | custom-call | tf_op jit(solution)/shard_map/attend_fwd/pallas_call | solution.py:98
  165.3 6.3 multiply_reduce_fusion.6
  174.0 7.0 %fusion.146 = f32[768,2560]{1,0:T(8,128)S(1)} fusion(bf16[768,960]{0,1:T(8,128)(2,1)S(1)} %multiply_convert_fusion.6, bf16[960,2560]{1,0:T(8,128)(2,1)} %bitcast.98), kind=kOutput, calls=%fused_computation.267 | convolution fusion | flops 3774873600 | bytes 14254080 | tf_op jit(solution)/shard_map/kd,df->kf/dot_general | solution.py:27
  181.1 7.8 %multiply_convert_fusion.2 = (bf16[768,2560]{1,0:T(8,128)(2,1)}, bf16[768,2560]{1,0:T(8,128)(2,1)}) fusion(f32[768,2560]{1,0:T(8,128)S(1)} %fusion.146, bf16[768,960]{0,1:T(8,128)(2,1)S(1)} %multiply_convert_fusion.6, bf16[960,2560]{1,0:T(8,128)(2,1)S(1)} %bitcast.138), kind=kOutput, calls=%fused_computation.25 | convolution fusion | flops 3788636160 | bytes 22118400 | tf_op jit(solution)/shard_map/kd,df->kf/dot_general | solution.py:27
  189.0 10.0 %multiply_add_fusion = (f32[768,960]{0,1:T(8,128)S(1)}, f32[768,960]{0,1:T(8,128)}) fusion(f32[1024,960]{0,1:T(8,128)S(1)} %copy-done.9, f32[768]{0:T(1024)S(1)} %get-tuple-element.203, f32[768,960]{0,1:T(8,128)S(1)} %copy-done.42, bf16[768,2560]{1,0:T(8,128)(2,1)} %get-tuple-element.182, bf16[2560,960]{1,0:T(8,128)(2,1)} %bitcast.154), kind=kOutput, calls=%fused_computation.90 | convolution fusion | flops 3777085440 | bytes 20646912 | tf_op jit(solution)/shard_map/kf,fd->kd/dot_general | solution.py:27
  199.7 4.0 fusion.106.qkv_ref
  206.8 19.9 %attend_fwd.4 = (bf16[512,960]{1,0:T(8,128)(2,1)}, bf16[15,512,64]{2,1,0:T(8,128)(2,1)}, bf16[5,512,64]{2,1,0:T(8,128)(2,1)}, bf16[5,512,64]{2,1,0:T(8,128)(2,1)}, f32[16,512]{1,0:T(8,128)}) custom-call(f32[512,1600]{1,0:T(8,128)} %fusion.106.qkv_ref, f32[512,128]{1,0:T(8,128)} %copy.145.cos_ref, f32[512,128]{1,0:T(8,128)} %copy.146.sin_ref, ...), custom_call_target="tpu_custom_call" | custom-call | tf_op jit(solution)/shard_map/attend_fwd/pallas_call | solution.py:98
  226.7 3.9 multiply_reduce_fusion.15
  230.9 3.0 fusion.147
  234.0 5.5 multiply_convert_fusion.5
  239.6 5.8 multiply_add_fusion.2
  245.8 2.6 fusion.104.qkv_ref
  253.7 8.0 %attend_fwd.5 = (bf16[256,960]{1,0:T(8,128)(2,1)}, bf16[15,256,64]{2,1,0:T(8,128)(2,1)}, bf16[5,256,64]{2,1,0:T(8,128)(2,1)}, bf16[5,256,64]{2,1,0:T(8,128)(2,1)}, f32[16,256]{1,0:T(8,128)}) custom-call(f32[256,1600]{1,0:T(8,128)} %fusion.104.qkv_ref, f32[256,128]{1,0:T(8,128)} %copy.148.cos_ref, f32[256,128]{1,0:T(8,128)} %copy.149.sin_ref, ...), custom_call_target="tpu_custom_call" | custom-call | tf_op jit(solution)/shard_map/attend_fwd/pallas_call | solution.py:98
  261.7 3.1 multiply_reduce_fusion.24
  271.3 3.2 multiply_reduce_fusion.23
  274.7 2.5 multiply_convert_fusion.9
  286.0 8.0 %attend_bwd.3 = bf16[256,1600]{1,0:T(8,128)(2,1)} custom-call(bf16[15,256,64]{2,1,0:T(8,128)(2,1)} %get-tuple-element.45.q_ref, bf16[5,256,64]{2,1,0:T(8,128)(2,1)} %get-tuple-element.46.k_ref, bf16[5,256,64]{2,1,0:T(8,128)(2,1)} %get-tuple-element.47.v_ref, f32[16,256]{1,0:T(8,128)} %get-tuple-element.48.lse_ref, bf16[256,960]{1,0:T(8,128)(2,1)} %copy.150.do_ref, ...), custom_call_target="tpu_custom_call" | custom-call | tf_op jit(solution)/shard_map/attend_bwd/pallas_call | solution.py:183
  294.0 4.0 multiply_reduce_fusion.20
  303.0 9.5 %multiply_convert_fusion.3 = (bf16[512,2560]{1,0:T(8,128)(2,1)S(1)}, bf16[512,2560]{1,0:T(8,128)(2,1)}) fusion(f32[512,2560]{1,0:T(8,128)} %copy-done.31, bf16[512,2560]{1,0:T(8,128)(2,1)S(1)} %copy-done.101, bf16[512,960]{0,1:T(8,128)(2,1)S(1)} %get-tuple-element.171, bf16[2560,960]{1,0:T(8,128)(2,1)} %bitcast.155), kind=kOutput, calls=%fused_computation.34 | convolution fusion | flops 2536243200 | bytes 19005440 | tf_op jit(solution)/shard_map/kd,fd->kf/dot_general | solution.py:27
  312.6 5.4 fusion.150
  318.1 3.1 multiply_reduce_fusion.10
  329.1 19.6 %attend_bwd.4 = bf16[512,1600]{1,0:T(8,128)(2,1)} custom-call(bf16[15,512,64]{2,1,0:T(8,128)(2,1)} %get-tuple-element.49.q_ref, bf16[5,512,64]{2,1,0:T(8,128)(2,1)} %get-tuple-element.50.k_ref, bf16[5,512,64]{2,1,0:T(8,128)(2,1)} %get-tuple-element.51.v_ref, f32[16,512]{1,0:T(8,128)} %get-tuple-element.52.lse_ref, bf16[512,960]{1,0:T(8,128)(2,1)} %copy.153.do_ref, ...), custom_call_target="tpu_custom_call" | custom-call | tf_op jit(solution)/shard_map/attend_bwd/pallas_call | solution.py:183
  348.8 4.9 multiply_reduce_fusion.11
  356.6 13.4 %multiply_convert_fusion = (bf16[768,2560]{1,0:T(8,128)(2,1)S(1)}, bf16[768,2560]{1,0:T(8,128)(2,1)}) fusion(f32[768,2560]{1,0:T(8,128)} %copy-done.94, bf16[768,2560]{1,0:T(8,128)(2,1)} %get-tuple-element.183, bf16[768,960]{0,1:T(8,128)(2,1)S(1)} %get-tuple-element.165, bf16[2560,960]{1,0:T(8,128)(2,1)} %bitcast.156), kind=kOutput, calls=%fused_computation.23 | convolution fusion | flops 3804364800 | bytes 26050560 | tf_op jit(solution)/shard_map/kd,fd->kf/dot_general | solution.py:27
  370.1 7.5 %fusion.151 = f32[768,960]{0,1:T(8,128)S(1)} fusion(bf16[768,2560]{1,0:T(8,128)(2,1)} %get-tuple-element.156, bf16[960,2560]{1,0:T(8,128)(2,1)S(1)} %bitcast.111), kind=kOutput, calls=%fused_computation.272 | convolution fusion | flops 3774873600 | bytes 11796480 | tf_op jit(solution)/shard_map/kf,df->kd/dot_general | solution.py:27
  377.7 4.5 multiply_reduce_fusion.1
  383.9 2.8 convolution_convert_fusion
  386.7 2.6 copy.156.do_ref
  390.7 35.8 %attend_bwd.5 = bf16[768,1600]{1,0:T(8,128)(2,1)} custom-call(bf16[15,768,64]{2,1,0:T(8,128)(2,1)} %get-tuple-element.53.q_ref, bf16[5,768,64]{2,1,0:T(8,128)(2,1)} %get-tuple-element.54.k_ref, bf16[5,768,64]{2,1,0:T(8,128)(2,1)} %get-tuple-element.55.v_ref, f32[16,768]{1,0:T(8,128)} %get-tuple-element.56.lse_ref, bf16[768,960]{1,0:T(8,128)(2,1)} %copy.156.do_ref, ...), custom_call_target="tpu_custom_call" | custom-call | tf_op jit(solution)/shard_map/attend_bwd/pallas_call | solution.py:183
  426.6 7.6 %multiply_reduce_fusion.2 = (f32[960]{0:T(1024)S(1)}, f32[768]{0:T(1024)S(1)}, f32[960]{0:T(1024)S(1)}, f32[768,960]{0,1:T(8,128)}) fusion(f32[1024,960]{0,1:T(8,128)S(1)} %copy-done.10, f32[768]{0:T(1024)S(1)} %copy-done.86, f32[960]{0:T(1024)S(1)} %mul.583, f32[768]{0:T(1024)S(1)} %subtract_multiply_fusion.3, bf16[768,1600]{1,0:T(8,128)(2,1)} %attend_bwd.5, ...), kind=kOutput, calls=%fused_computation.83 | convolution fusion | flops 2365191424 | bytes 11669760 | tf_op jit(solution)/shard_map/ke,de->kd/dot_general | solution.py:27
  434.9 11.9 %fusion.21 = bf16[2560,960]{0,1:T(8,128)(2,1)} fusion(bf16[768,2560]{1,0:T(8,128)(2,1)} %get-tuple-element.182, bf16[512,2560]{1,0:T(8,128)(2,1)} %get-tuple-element.187, bf16[256,2560]{1,0:T(8,128)(2,1)} %copy-done.60, bf16[768,960]{0,1:T(8,128)(2,1)S(1)} %copy-done.59, bf16[512,960]{0,1:T(8,128)(2,1)} %copy-done.65, bf16[256,960]{0,1:T(8,128)(2,1)S(1)} %copy-done.76), kind=kOutput, calls=%fused_computation.28 | convolution fusion | flops 7584645120 | bytes 15728640 | tf_op jit(solution)/shard_map/kd,ke->de/dot_general | solution.py:27
  446.8 8.0 %copy.159 = bf16[2560,960]{1,0:T(8,128)(2,1)} copy(bf16[2560,960]{0,1:T(8,128)(2,1)} %fusion.21) | data formatting | bytes 9830400 | tf_op jit(solution)/shard_map/convert_element_type | solution.py:811
  454.8 12.2 %fusion.24 = bf16[960,2560]{1,0:T(8,128)(2,1)} fusion(bf16[768,2560]{1,0:T(8,128)(2,1)} %copy-done.98, bf16[512,2560]{1,0:T(8,128)(2,1)} %copy-done.99, bf16[256,2560]{1,0:T(8,128)(2,1)} %copy-done.95, bf16[768,960]{0,1:T(8,128)(2,1)} %copy-done.56, bf16[512,960]{0,1:T(8,128)(2,1)S(1)} %copy-done.33, bf16[256,960]{0,1:T(8,128)(2,1)S(1)} %copy-done.40), kind=kOutput, calls=%fused_computation.29 | convolution fusion | flops 7584645120 | bytes 15728640 | tf_op jit(solution)/shard_map/kd,ke->de/dot_general | solution.py:27
  467.1 9.6 %fusion.27 = bf16[960,2560]{1,0:T(8,128)(2,1)} fusion(bf16[768,2560]{1,0:T(8,128)(2,1)S(1)} %copy-done.102, bf16[512,2560]{1,0:T(8,128)(2,1)S(1)} %copy-done.100, bf16[256,2560]{1,0:T(8,128)(2,1)S(1)} %copy-done.97, bf16[768,960]{0,1:T(8,128)(2,1)S(1)} %copy-done.57, bf16[512,960]{0,1:T(8,128)(2,1)S(1)} %copy-done.33, bf16[256,960]{0,1:T(8,128)(2,1)S(1)} %copy-done.40), kind=kOutput, calls=%fused_computation.30 | convolution fusion | flops 7584645120 | bytes 15728640 | tf_op jit(solution)/shard_map/kd,ke->de/dot_general | solution.py:27
  476.9 3.6 fusion.87
  480.6 5.5 fusion.44
  486.1 4.0 pad_maximum_fusion
  490.1 160.5 %reduce_grads.1 = (bf16[2,120,2560]{2,1,0:T(8,128)(2,1)}, bf16[2,120,2560]{2,1,0:T(8,128)(2,1)}, bf16[2,120,2560]{2,1,0:T(8,128)(2,1)}, bf16[2,320,960]{2,1,0:T(8,128)(2,1)}, f32[8,1024]{1,0:T(8,128)}) custom-call(bf16[4,2,120,2560]{3,2,1,0:T(8,128)(2,1)} %bitcast.153, bf16[4,2,120,2560]{3,2,1,0:T(8,128)(2,1)} %bitcast.165, ...), custom_call_target="tpu_custom_call" | custom-call | tf_op jit(solution)/shard_map/reduce_grads/pallas_call | solution.py:695
  650.6 3.1 bitcast_convert_fusion
  653.7 3.3 copy.162
  660.9 3.2 bitcast_convert_fusion.1
  664.0 3.0 bitcast_convert_fusion.2
  669.8 5.3 add_convert_fusion
  676.4 3.6 fusion.95
  683.8 3.5 fusion.92
  (392 shorter events, 84.8 us)
Async XLA Ops:
  4.3 264.7 %copy-start.92 = (s32[1024]{0:T(1024)}, s32[1024]{0:T(1024)S(1)}, u32[]{:S(2)}) copy-start(s32[1024]{0:T(1024)S(1)} %fusion.113) | copy-start | bytes 12292
  125.5 39.8 %copy-start.43 = (f32[1024,128]{0,1:T(8,128)}, f32[1024,128]{0,1:T(8,128)S(1)}, u32[]{:S(2)}) copy-start(f32[1024,128]{0,1:T(8,128)S(1)} %get-tuple-element.204) | copy-start | bytes 1572868
  129.1 36.2 %copy-start.8 = (f32[1024,960]{0,1:T(8,128)S(1)}, f32[1024,960]{0,1:T(8,128)}, u32[]{:S(2)}) copy-start(f32[1024,960]{0,1:T(8,128)} %fusion.42) | copy-start | bytes 11796484
  171.6 9.4 %copy-start.79 = (f32[768]{0:T(1024)}, f32[768]{0:T(1024)S(1)}, u32[]{:S(2)}) copy-start(f32[768]{0:T(1024)S(1)} %add_rsqrt_fusion) | copy-start | bytes 9220
  171.7 9.3 %slice-start.16 = ((s8[4915200]{0:T(1024)(128)(4,1)}), s8[4194304]{0:T(1024)(128)(4,1)S(1)}, s32[]{:S(2)}) async-start(s8[4915200]{0:T(1024)(128)(4,1)} %bitcast.136), calls=%async_computation.16 | async-start | bytes 8388608
  188.9 10.8 %slice-start.8 = ((s8[4915200]{0:T(1024)(128)(4,1)}), s8[4194304]{0:T(1024)(128)(4,1)S(1)}, s32[]{:S(2)}) async-start(s8[4915200]{0:T(1024)(128)(4,1)} %bitcast.120), calls=%async_computation.8 | async-start | bytes 8388608
  189.0 10.6 %slice-start.9 = ((s8[4915200]{0:T(1024)(128)(4,1)}), s8[720896]{0:T(1024)(128)(4,1)S(1)}, s32[]{:S(2)}) async-start(s8[4915200]{0:T(1024)(128)(4,1)} %bitcast.120), calls=%async_computation.9 | async-start | bytes 1441792
  230.9 8.6 %slice-start.26 = ((s8[5242880]{0:T(1024)(128)(4,1)}), s8[4194304]{0:T(1024)(128)(4,1)S(1)}, s32[]{:S(2)}) async-start(s8[5242880]{0:T(1024)(128)(4,1)} %bitcast.157), calls=%async_computation.26 | async-start | bytes 8388608
  230.9 14.9 %slice-start.10 = ((s8[4915200]{0:T(1024)(128)(4,1)}), s8[4194304]{0:T(1024)(128)(4,1)S(1)}, s32[]{:S(2)}) async-start(s8[4915200]{0:T(1024)(128)(4,1)} %bitcast.123), calls=%async_computation.10 | async-start | bytes 8388608
  234.0 11.8 %slice-start.11 = ((s8[4915200]{0:T(1024)(128)(4,1)}), s8[720896]{0:T(1024)(128)(4,1)S(1)}, s32[]{:S(2)}) async-start(s8[4915200]{0:T(1024)(128)(4,1)} %bitcast.123), calls=%async_computation.11 | async-start | bytes 1441792
  245.8 19.2 %slice-start.2 = ((s8[4915200]{0:T(1024)(128)(4,1)}), s8[720896]{0:T(1024)(128)(4,1)S(1)}, s32[]{:S(2)}) async-start(s8[4915200]{0:T(1024)(128)(4,1)} %bitcast.102), calls=%async_computation.2 | async-start | bytes 1441792
  253.7 11.3 %slice-start.3 = ((s8[4915200]{0:T(1024)(128)(4,1)}), s8[4194304]{0:T(1024)(128)(4,1)S(1)}, s32[]{:S(2)}) async-start(s8[4915200]{0:T(1024)(128)(4,1)} %bitcast.102), calls=%async_computation.3 | async-start | bytes 8388608
  264.8 15.5 %copy-start.20 = (f32[256,960]{0,1:T(8,128)}, f32[256,960]{0,1:T(8,128)S(1)}, u32[]{:S(2)}) copy-start(f32[256,960]{0,1:T(8,128)S(1)} %get-tuple-element.150) | copy-start | bytes 2949124
  271.3 9.0 %copy-start.23 = (f32[1024,960]{0,1:T(8,128)}, f32[1024,960]{0,1:T(8,128)S(1)}, u32[]{:S(2)}) copy-start(f32[1024,960]{0,1:T(8,128)S(1)} %fusion.40) | copy-start | bytes 11796484
  284.7 9.3 %copy-start.26 = (f32[512,960]{0,1:T(8,128)S(1)}, f32[512,960]{0,1:T(8,128)}, u32[]{:S(2)}) copy-start(f32[512,960]{0,1:T(8,128)} %copy-done.25) | copy-start | bytes 5898244
  284.8 13.3 %copy-start.51 = (f32[64,1024]{1,0:T(8,128)}, f32[64,1024]{1,0:T(8,128)S(1)}, u32[]{:S(2)}) copy-start(f32[64,1024]{1,0:T(8,128)S(1)} %get-tuple-element.206) | copy-start | bytes 786436
  298.2 19.8 %slice-start.22 = ((s8[4915200]{0:T(1024)(128)(4,1)}), s8[4194304]{0:T(1024)(128)(4,1)S(1)}, s32[]{:S(2)}) async-start(s8[4915200]{0:T(1024)(128)(4,1)} %bitcast.146), calls=%async_computation.22 | async-start | bytes 8388608
  300.1 21.1 %copy-start.16 = (f32[256,960]{0,1:T(8,128)}, f32[256,960]{0,1:T(8,128)S(1)}, u32[]{:S(2)}) copy-start(f32[256,960]{0,1:T(8,128)S(1)} %get-tuple-element.163) | copy-start | bytes 2949124
  300.1 12.4 %slice-start.4 = ((s8[4915200]{0:T(1024)(128)(4,1)}), s8[4194304]{0:T(1024)(128)(4,1)S(1)}, s32[]{:S(2)}) async-start(s8[4915200]{0:T(1024)(128)(4,1)} %bitcast.106), calls=%async_computation.4 | async-start | bytes 8388608
  300.6 11.9 %copy-start.65 = (bf16[512,960]{0,1:T(8,128)(2,1)}, bf16[512,960]{0,1:T(8,128)(2,1)S(1)}, u32[]{:S(2)}) copy-start(bf16[512,960]{0,1:T(8,128)(2,1)S(1)} %get-tuple-element.171) | copy-start | bytes 2949124
  303.0 9.6 %slice-start.5 = ((s8[4915200]{0:T(1024)(128)(4,1)}), s8[720896]{0:T(1024)(128)(4,1)S(1)}, s32[]{:S(2)}) async-start(s8[4915200]{0:T(1024)(128)(4,1)} %bitcast.106), calls=%async_computation.5 | async-start | bytes 1441792
  303.0 15.0 %slice-start.23 = ((s8[4915200]{0:T(1024)(128)(4,1)}), s8[720896]{0:T(1024)(128)(4,1)S(1)}, s32[]{:S(2)}) async-start(s8[4915200]{0:T(1024)(128)(4,1)} %bitcast.146), calls=%async_computation.23 | async-start | bytes 1441792
  312.5 10.9 %slice-start.12 = ((s8[4915200]{0:T(1024)(128)(4,1)}), s8[4194304]{0:T(1024)(128)(4,1)S(1)}, s32[]{:S(2)}) async-start(s8[4915200]{0:T(1024)(128)(4,1)} %bitcast.126), calls=%async_computation.12 | async-start | bytes 8388608
  329.1 19.6 %copy-start.15 = (f32[768,960]{0,1:T(8,128)S(1)}, f32[768,960]{0,1:T(8,128)}, u32[]{:S(2)}) copy-start(f32[768,960]{0,1:T(8,128)} %copy-done.13) | copy-start | bytes 8847364
  355.0 27.2 %copy-start.11 = (f32[512,960]{0,1:T(8,128)}, f32[512,960]{0,1:T(8,128)S(1)}, u32[]{:S(2)}) copy-start(f32[512,960]{0,1:T(8,128)S(1)} %multiply_add_fusion.1) | copy-start | bytes 5898244
  355.8 14.2 %slice-start.6 = ((s8[4915200]{0:T(1024)(128)(4,1)}), s8[4194304]{0:T(1024)(128)(4,1)S(1)}, s32[]{:S(2)}) async-start(s8[4915200]{0:T(1024)(128)(4,1)} %bitcast.109), calls=%async_computation.6 | async-start | bytes 8388608
  355.8 21.8 %slice-start.24 = ((s8[4915200]{0:T(1024)(128)(4,1)}), s8[4194304]{0:T(1024)(128)(4,1)S(1)}, s32[]{:S(2)}) async-start(s8[4915200]{0:T(1024)(128)(4,1)} %bitcast.149), calls=%async_computation.24 | async-start | bytes 8388608
  356.6 13.4 %copy-start.58 = (bf16[768,960]{0,1:T(8,128)(2,1)}, bf16[768,960]{0,1:T(8,128)(2,1)S(1)}, u32[]{:S(2)}) copy-start(bf16[768,960]{0,1:T(8,128)(2,1)S(1)} %get-tuple-element.165) | copy-start | bytes 4423684
  356.6 13.4 %slice-start.7 = ((s8[4915200]{0:T(1024)(128)(4,1)}), s8[720896]{0:T(1024)(128)(4,1)S(1)}, s32[]{:S(2)}) async-start(s8[4915200]{0:T(1024)(128)(4,1)} %bitcast.109), calls=%async_computation.7 | async-start | bytes 1441792
  356.6 21.0 %slice-start.25 = ((s8[4915200]{0:T(1024)(128)(4,1)}), s8[720896]{0:T(1024)(128)(4,1)S(1)}, s32[]{:S(2)}) async-start(s8[4915200]{0:T(1024)(128)(4,1)} %bitcast.149), calls=%async_computation.25 | async-start | bytes 1441792
  370.1 13.8 %slice-start.14 = ((s8[4915200]{0:T(1024)(128)(4,1)}), s8[4194304]{0:T(1024)(128)(4,1)S(1)}, s32[]{:S(2)}) async-start(s8[4915200]{0:T(1024)(128)(4,1)} %bitcast.129), calls=%async_computation.14 | async-start | bytes 8388608
  390.6 35.9 %copy-start.82 = (f32[768]{0:T(1024)S(1)}, f32[768]{0:T(1024)}, u32[]{:S(2)}) copy-start(f32[768]{0:T(1024)} %copy-done.81) | copy-start | bytes 9220
  390.7 35.9 %copy-start.10 = (f32[1024,960]{0,1:T(8,128)S(1)}, f32[1024,960]{0,1:T(8,128)}, u32[]{:S(2)}) copy-start(f32[1024,960]{0,1:T(8,128)} %fusion.42) | copy-start | bytes 11796484
  390.7 35.9 %copy-start.86 = (f32[768]{0:T(1024)S(1)}, f32[768]{0:T(1024)}, u32[]{:S(2)}) copy-start(f32[768]{0:T(1024)} %copy-done.85) | copy-start | bytes 9220
  426.5 8.3 %copy-start.59 = (bf16[768,960]{0,1:T(8,128)(2,1)S(1)}, bf16[768,960]{0,1:T(8,128)(2,1)}, u32[]{:S(2)}) copy-start(bf16[768,960]{0,1:T(8,128)(2,1)} %copy-done.58) | copy-start | bytes 4423684
  426.6 8.3 %copy-start.76 = (bf16[256,960]{0,1:T(8,128)(2,1)S(1)}, bf16[256,960]{0,1:T(8,128)(2,1)}, u32[]{:S(2)}) copy-start(bf16[256,960]{0,1:T(8,128)(2,1)} %copy-done.75) | copy-start | bytes 1474564
  454.7 12.3 %copy-start.57 = (bf16[768,960]{0,1:T(8,128)(2,1)S(1)}, bf16[768,960]{0,1:T(8,128)(2,1)}, u32[]{:S(2)}) copy-start(bf16[768,960]{0,1:T(8,128)(2,1)} %copy-done.56) | copy-start | bytes 4423684
  454.8 12.3 %copy-start.97 = (bf16[256,2560]{1,0:T(8,128)(2,1)S(1)}, bf16[256,2560]{1,0:T(8,128)(2,1)}, u32[]{:S(2)}) copy-start(bf16[256,2560]{1,0:T(8,128)(2,1)} %copy-done.96) | copy-start | bytes 3932164
  454.8 12.3 %copy-start.100 = (bf16[512,2560]{1,0:T(8,128)(2,1)S(1)}, bf16[512,2560]{1,0:T(8,128)(2,1)}, u32[]{:S(2)}) copy-start(bf16[512,2560]{1,0:T(8,128)(2,1)} %get-tuple-element.158) | copy-start | bytes 7864324
  454.8 12.3 %copy-start.102 = (bf16[768,2560]{1,0:T(8,128)(2,1)S(1)}, bf16[768,2560]{1,0:T(8,128)(2,1)}, u32[]{:S(2)}) copy-start(bf16[768,2560]{1,0:T(8,128)(2,1)} %get-tuple-element.156) | copy-start | bytes 11796484
  467.0 9.7 %copy-start.53 = (bf16[768,960]{1,0:T(8,128)(2,1)S(1)}, bf16[768,960]{1,0:T(8,128)(2,1)}, u32[]{:S(2)}) copy-start(bf16[768,960]{1,0:T(8,128)(2,1)} %get-tuple-element.39) | copy-start | bytes 4423684
  467.1 9.7 %copy-start.55 = (bf16[768,960]{0,1:T(8,128)(2,1)S(1)}, bf16[768,960]{0,1:T(8,128)(2,1)}, u32[]{:S(2)}) copy-start(bf16[768,960]{0,1:T(8,128)(2,1)} %copy-done.54) | copy-start | bytes 4423684
  467.1 9.7 %copy-start.62 = (bf16[512,960]{1,0:T(8,128)(2,1)S(1)}, bf16[512,960]{1,0:T(8,128)(2,1)}, u32[]{:S(2)}) copy-start(bf16[512,960]{1,0:T(8,128)(2,1)} %get-tuple-element.43) | copy-start | bytes 2949124
  467.1 9.7 %copy-start.64 = (bf16[512,960]{0,1:T(8,128)(2,1)S(1)}, bf16[512,960]{0,1:T(8,128)(2,1)}, u32[]{:S(2)}) copy-start(bf16[512,960]{0,1:T(8,128)(2,1)} %copy-done.63) | copy-start | bytes 2949124
  467.1 9.7 %copy-start.67 = (bf16[256,960]{1,0:T(8,128)(2,1)S(1)}, bf16[256,960]{1,0:T(8,128)(2,1)}, u32[]{:S(2)}) copy-start(bf16[256,960]{1,0:T(8,128)(2,1)} %get-tuple-element.44) | copy-start | bytes 1474564
  467.1 9.7 %copy-start.74 = (bf16[256,960]{0,1:T(8,128)(2,1)S(1)}, bf16[256,960]{0,1:T(8,128)(2,1)}, u32[]{:S(2)}) copy-start(bf16[256,960]{0,1:T(8,128)(2,1)} %copy-done.73) | copy-start | bytes 1474564
  660.9 9.0 %copy-start.12 = (f32[512,960]{0,1:T(8,128)S(1)}, f32[512,960]{0,1:T(8,128)}, u32[]{:S(2)}) copy-start(f32[512,960]{0,1:T(8,128)} %copy-done.11) | copy-start | bytes 5898244
  660.9 9.0 %copy-start.84 = (f32[960,1]{0,1:T(1,128)S(1)}, f32[960,1]{0,1:T(1,128)}, u32[]{:S(2)}) copy-start(f32[960,1]{0,1:T(1,128)} %copy-done.83) | copy-start | bytes 11524
  (85 other events, 343.1 us)
